TPU v7x, 32 devices: a whole 2x2x4 slice. The times are simulated.
32 devices in a mesh: rep: 4 (over y, x), fsdp: 8 (over z, core).
Axes of the slice: x: 2, y: 2, z: 4, core: 2. Of those that a mesh axis runs over, the one named last changes fastest.
Arguments:
- tokens: bfloat16 [4, 4096, 1024], P('rep', 'fsdp'), may hold values from -6 to 6
- image_ids: int32 [4, 4096], P('rep', 'fsdp'), may hold values from 0 to 4, never falling along the last dimension, each value on 1 to 1024 neighbouring positions
- ln1_gain: bfloat16 [1024], P('fsdp'), may hold values from 0.099609375 to 1.8984375
- ln1_bias: bfloat16 [1024], P('fsdp'), may hold values from -3 to 3
- qkv_weight: bfloat16 [1024, 3072], P('fsdp'), may hold values from -0.1875 to 0.1875
- query_bias: bfloat16 [1024], P('fsdp'), may hold values from -3 to 3
- value_bias: bfloat16 [1024], P('fsdp'), may hold values from -3 to 3
- proj_weight: bfloat16 [1024, 1024], P('fsdp'), may hold values from -1.5 to 1.5
- proj_bias: bfloat16 [1024], P('fsdp'), may hold values from -3 to 3
- scale_attn: bfloat16 [1024], P('fsdp'), may hold values from 0.5 to 1.5
- ln2_gain: bfloat16 [1024], P('fsdp'), may hold values from 0.099609375 to 1.8984375
- ln2_bias: bfloat16 [1024], P('fsdp'), may hold values from -3 to 3
- fc1_weight: bfloat16 [1024, 4096], P('fsdp'), may hold values from -0.1875 to 0.1875
- fc1_bias: bfloat16 [4096], P('fsdp'), may hold values from -3 to 3
- fc2_weight: bfloat16 [4096, 1024], P('fsdp'), may hold values from -0.09375 to 0.09375
- fc2_bias: bfloat16 [1024], P('fsdp'), may hold values from -3 to 3
- scale_mlp: bfloat16 [1024], P('fsdp'), may hold values from 0.5 to 1.5
- cotangent: bfloat16 [4, 4096, 1024], P('rep', 'fsdp'), may hold values from -6 to 6
Outputs:
- output: bfloat16 [4, 4096, 1024], P('rep', 'fsdp')
- input_grad: float32 [4, 4096, 1024], P('rep', 'fsdp')
- grad_ln1_gain: float32 [1024], P('fsdp')
- grad_ln1_bias: float32 [1024], P('fsdp')
- grad_qkv_weight: float32 [1024, 3072], P('fsdp')
- grad_query_bias: float32 [1024], P('fsdp')
- grad_value_bias: float32 [1024], P('fsdp')
- grad_proj_weight: float32 [1024, 1024], P('fsdp')
- grad_proj_bias: float32 [1024], P('fsdp')
- grad_scale_attn: float32 [1024], P('fsdp')
- grad_ln2_gain: float32 [1024], P('fsdp')
- grad_ln2_bias: float32 [1024], P('fsdp')
- grad_fc1_weight: float32 [1024, 4096], P('fsdp')
- grad_fc1_bias: float32 [4096], P('fsdp')
- grad_fc2_weight: float32 [4096, 1024], P('fsdp')
- grad_fc2_bias: float32 [1024], P('fsdp')
- grad_scale_mlp: float32 [1024], P('fsdp')
Inputs may be any that keep to these rules, and one draw needn't show every extreme that they name: `image_ids`: within each replica group the image numbers never fall along the tokens, every number from 0 up is used, and each image holds 1 to 1024 tokens, one of them exactly 1024.
All inputs are finite; a program needn't handle non-finite values.
Results may differ from a plain program's by a relative error of at most 0.012.
The roundings to bfloat16 on the way count: a program that leaves them out, or rounds other values in their place, can miss the bound.
Values may be sent and summed in bfloat16 or wider, within the bound.
No kernel may reach another device: no remote copies, remote signals or barrier semaphores. Data moves between devices by JAX's collectives and lax.ppermute only.
A program may use at most 256 MiB of HBM per device.

v0:
```python
import functools
import math

import jax
import jax.numpy as jnp
from jax import lax
from jax.experimental import pallas as pl
from jax.experimental.pallas import tpu as pltpu
from jax.sharding import PartitionSpec as P

D = 1024
HEADS = 16
HEAD_DIM = 64
LANES = 128

EPSILON = 1e-06
MASKED = -1e30
BLOCK = 256

SHORT = pl.CostEstimate(flops=1, transcendentals=0, bytes_accessed=1)

f32 = jnp.float32
bf16 = jnp.bfloat16


def normalize(features):
    row_mean = jnp.mean(features, axis=-1, keepdims=True)
    centred = features - row_mean
    variance = jnp.mean(centred * centred, axis=-1, keepdims=True)
    inverse = lax.rsqrt(variance + EPSILON)
    return centred * inverse, inverse


def norm_back(gradient, normal, inverse, gain_vec):
    scaled = gradient * gain_vec
    mean_first = jnp.mean(scaled, axis=-1, keepdims=True)
    mean_second = jnp.mean(scaled * normal, axis=-1, keepdims=True)
    return inverse * (scaled - mean_first - normal * mean_second)


def gelu_pair(values):
    cumulative = 0.5 * (1.0 + lax.erf(values * 2.0 ** (-0.5)))
    density = jnp.exp(-0.5 * values * values) * (2.0 * math.pi) ** (-0.5)
    return (values * cumulative, cumulative + values * density)


def dot(a, b):
    return jnp.dot(a, b, preferred_element_type=f32)


def dot_nt(a, b):
    return lax.dot_general(a, b, (((1,), (1,)), ((), ())), preferred_element_type=f32)


def dot_tn(a, b):
    return lax.dot_general(a, b, (((0,), (0,)), ((), ())), preferred_element_type=f32)


def swap_cores(value):
    size = lax.axis_size("fsdp")
    return lax.ppermute(value, "fsdp", [(i, i ^ 1) for i in range(size)])


def along_z(value, by):
    size = lax.axis_size("fsdp")
    return lax.ppermute(value, "fsdp", [(i, (i + 2 * by) % size) for i in range(size)])


def from_chip(value, by):
    size = lax.axis_size("fsdp")
    pairs = [(i, i + 2 * by) for i in range(size) if 0 <= i + 2 * by < size]
    return lax.ppermute(value, "fsdp", pairs)


def across_rep(value, bit):
    size = lax.axis_size("rep")
    return lax.ppermute(value, "rep", [(i, i ^ (1 << bit)) for i in range(size)])


def pick(value, index, axis):
    return lax.dynamic_index_in_dim(value, index, axis, keepdims=False)


def rep_bits():
    return lax.axis_size("rep").bit_length() - 1


def tie(*values):
    return lax.optimization_barrier(values)


def settle(value, *fields):
    held = [getattr(o, name) for o, name in fields]
    value, held = lax.optimization_barrier((value, held))
    for (o, name), new in zip(fields, held):
        setattr(o, name, new)
    return value


def fetch_z(own):
    return [own] + [along_z(own, k) for k in range(1, lax.axis_size("fsdp") // 2)]


class Gather:
    def __init__(self, pieces, rows, name):
        self.rows, self.cols, self.name = rows, pieces[0].shape[1], name
        half = rows // 2
        bits = list(range(rep_bits()))
        self.orders = [bits, bits[::-1]]
        self.parts = [
            [(jnp.stack([p[:half] for p in pieces])[None], [0])],
            [(jnp.stack([p[half:rows] for p in pieces])[None], [0])],
        ]
        self.at = 0

    def send(self, *values):
        whole = [
            (ps[0][0] if len(ps) == 1 else jnp.concatenate([a for a, _ in ps]), [o for _, os in ps for o in os])
            for ps in self.parts
        ]
        values, arrays = lax.optimization_barrier((values, [a for a, _ in whole]))
        self.parts = []
        for array, (_, offsets), order in zip(arrays, whole, self.orders):
            flip = 1 << order[self.at]
            received = across_rep(array, order[self.at])
            self.parts.append([(array, offsets), (received, [o ^ flip for o in offsets])])
        self.at += 1
        return values[0] if len(values) == 1 else values

    def arrive(self, value):
        value, arrays = lax.optimization_barrier((value, [a for ps in self.parts for a, _ in ps]))
        self.parts = [[(arrays.pop(0), o) for _, o in ps] for ps in self.parts]
        return value

    def assemble(self, here, rank, tail_rows=0):
        depth, ranks = lax.axis_size("fsdp") // 2, lax.axis_size("rep")
        sources, plan = [], []
        for number, parts in enumerate(self.parts):
            for array, offsets in parts:
                sources.append(array)
                plan.append((number, offsets))
        dtype = sources[0].dtype
        shape = (depth * self.rows, ranks * self.cols)
        shapes = [jax.ShapeDtypeStruct(shape, dtype)]
        if tail_rows:
            tail = shape[1] // 4
            shapes = [
                jax.ShapeDtypeStruct((shape[0], shape[1] - tail), dtype),
                jax.ShapeDtypeStruct((depth * tail_rows, 2 * tail), dtype),
            ]
        out = pl.pallas_call(
            functools.partial(assemble_kernel, plan, depth, self.rows, self.cols, tail_rows),
            out_shape=shapes,
            grid_spec=pltpu.PrefetchScalarGridSpec(
                num_scalar_prefetch=1,
                grid=(1,),
                in_specs=[pl.BlockSpec(memory_space=pl.ANY)] * len(sources),
                out_specs=[pl.BlockSpec(memory_space=pl.ANY)] * len(shapes),
                scratch_shapes=[
                    pltpu.VMEM(shape, dtype),
                    pltpu.SemaphoreType.DMA((2 * ranks * depth,)),
                    pltpu.SemaphoreType.DMA((3 * depth,)),
                ],
            ),
            compiler_params=pltpu.CompilerParams(vmem_limit_bytes=16 << 20),
            cost_estimate=SHORT,
            name=self.name,
        )(jnp.stack([here, rank]).astype(jnp.int32), *sources)
        return out if tail_rows else out[0]


def assemble_kernel(plan, depth, rows, cols, tail_rows, index_ref, *refs):
    count = len(plan)
    sources = refs[:count]
    targets = refs[count : count + (2 if tail_rows else 1)]
    held, in_sems, out_sems = refs[-3:]
    here, rank = index_ref[0], index_ref[1]
    half = rows // 2
    waits = [[] for _ in range(depth)]
    number = 0
    for k in range(depth):
        place = lax.rem(here - k + depth, depth)
        for which, (colour, offsets) in enumerate(plan):
            for m, offset in enumerate(offsets):
                at_row = pl.multiple_of(place * rows + colour * half, half)
                at_col = pl.multiple_of((rank ^ offset) * cols, cols)
                copy = pltpu.make_async_copy(
                    sources[which].at[m, k],
                    held.at[pl.ds(at_row, half), pl.ds(at_col, cols)],
                    in_sems.at[number],
                )
                copy.start()
                waits[k].append(copy)
                number += 1
    outs = []
    main = targets[0].shape[1]
    for k in range(depth):
        place = lax.rem(here - k + depth, depth)
        for copy in waits[k]:
            copy.wait()
        base = pl.multiple_of(place * rows, rows)
        band = pl.ds(base, rows)
        out = pltpu.make_async_copy(held.at[band, pl.ds(0, main)], targets[0].at[band], out_sems.at[3 * k])
        out.start()
        outs.append(out)
        if tail_rows:
            wide = targets[1].shape[1] // 2
            for side in range(2):
                out = pltpu.make_async_copy(
                    held.at[pl.ds(base + side * tail_rows, tail_rows), pl.ds(main, wide)],
                    targets[1].at[
                        pl.ds(pl.multiple_of(place * tail_rows, tail_rows), tail_rows),
                        pl.ds(side * wide, wide),
                    ],
                    out_sems.at[3 * k + 1 + side],
                )
                out.start()
                outs.append(out)
    for out in outs:
        out.wait()


def halves(ranks, bit, held):
    flip = 1 << bit
    kept = [o for o in held if not o & flip]
    return kept, [o ^ flip for o in kept]


def relative_blocks(grads, rank, orders):
    depth, ranks = lax.axis_size("fsdp") // 2, lax.axis_size("rep")
    width = grads.shape[1] // ranks
    rows = grads.shape[0] // depth
    shaped = grads.reshape(depth, rows, grads.shape[1])
    share = rows // len(orders)
    first = []
    for n, order in enumerate(orders):
        block = lambda o: lax.dynamic_slice(
            shaped, (0, n * share, (rank ^ o) * width), (depth, share, width)
        )
        kept, given = halves(ranks, order[0], list(range(ranks)))
        first.append((jnp.stack([block(o) for o in kept]), jnp.stack([block(o) for o in given])))
    return first


class Reduce:
    def __init__(self, first, here, orders):
        self.here, self.orders, self.at = here, orders, 0
        ranks = lax.axis_size("rep")
        self.held = []
        for (keep, give), order in zip(first, orders):
            kept, given = halves(ranks, order[0], list(range(ranks)))
            self.held.append((kept, keep, give))

    def send(self, *values):
        values, gives = lax.optimization_barrier((values, [give for _, _, give in self.held]))
        self.received = [across_rep(g, order[self.at]) for g, order in zip(gives, self.orders)]
        self.at += 1
        return values[0] if len(values) == 1 else values

    def arrive(self, *values):
        values, received = lax.optimization_barrier((values, self.received))
        held = []
        for (kept, keep, _), got, order in zip(self.held, received, self.orders):
            total = (keep.astype(f32) + got.astype(f32)).astype(bf16)
            if self.at < len(order):
                stay, leave = halves(None, order[self.at], kept)
                take = lambda os: jnp.stack([total[kept.index(o)] for o in os])
                held.append((stay, take(stay), take(leave)))
            else:
                held.append((kept, total[0], None))
        self.held = held
        return values[0] if len(values) == 1 else values

    def send_z(self, *values, extra=None):
        depth = lax.axis_size("fsdp") // 2
        parts = [keep for _, keep, _ in self.held]
        whole = parts[0] if len(parts) == 1 else jnp.concatenate(parts, axis=1)
        if extra is not None:
            whole = jnp.concatenate([whole, extra], axis=1)
        pieces = [pick(whole, lax.rem(self.here + k, depth), 0) for k in range(depth)]
        values, pieces = lax.optimization_barrier((values, pieces))
        self.pieces = [pieces[0]] + [along_z(p, k) for k, p in enumerate(pieces) if k]
        return values[0] if len(values) == 1 else values

    def arrive_z(self, *values):
        values, pieces = lax.optimization_barrier((values, self.pieces))
        total = pieces[0].astype(f32)
        for piece in pieces[1:]:
            total = total + piece.astype(f32)
        self.total = total
        return values[0] if len(values) == 1 else values


class Spread:
    def __init__(self, value):
        bits = list(range(rep_bits()))
        self.orders = [bits, bits[::-1]]
        half = value.shape[0] // 2
        self.arrays = [value[:half][None], value[half:][None]]
        self.offsets = [[0], [0]]
        self.at = 0

    def send(self, *values):
        values, arrays = lax.optimization_barrier((values, self.arrays))
        self.arrays = []
        for n, (array, order) in enumerate(zip(arrays, self.orders)):
            flip = 1 << order[self.at]
            received = across_rep(array, order[self.at])
            self.arrays.append(jnp.concatenate([array, received]))
            self.offsets[n] = self.offsets[n] + [o ^ flip for o in self.offsets[n]]
        self.at += 1
        return values[0] if len(values) == 1 else values

    def blocks(self, rank, start, size):
        return jnp.concatenate(
            [rep_blocks(a[:, :, start : start + size], o, rank) for a, o in zip(self.arrays, self.offsets)]
        )


def rep_blocks(stacked, offsets, rank):
    blocks = []
    for i in range(len(offsets)):
        block = stacked[0]
        for entry, offset in enumerate(offsets):
            block = jnp.where((rank ^ offset) == i, stacked[entry], block)
        blocks.append(block)
    return jnp.concatenate(blocks, axis=1)


def share_kernel(widths, index_ref, qkv_ref, proj_ref, fc1_ref, keep_ref, give_ref, sems):
    rank, core = index_ref[0], index_ref[1]
    wide1, wide2, block, unit, half = widths
    is_proj = rank * wide1 >= 3 * half

    def copies(second):
        made = []
        for out, (ref, which) in enumerate(((keep_ref, core), (give_ref, 1 - core))):
            for c in range(wide1 // block):
                col = rank * wide1 + c * block
                if second:
                    source, at = proj_ref, which * half + col - 3 * half
                else:
                    source, at = qkv_ref, 2 * col + which * block
                made.append((source, at, block, ref, c * block))
        return made

    def run(plan, first):
        started = []
        for n, (source, at, size, ref, to) in enumerate(plan):
            copy = pltpu.make_async_copy(
                source.at[:, pl.ds(pl.multiple_of(at, LANES), size)], ref.at[:, pl.ds(to, size)], sems.at[first + n]
            )
            copy.start()
            started.append(copy)
        return started

    col = rank * wide2
    plan2 = []
    for ref, which in ((keep_ref, core), (give_ref, 1 - core)):
        at = col + (lax.div(col, unit) + which) * unit
        plan2.append((fc1_ref, at, wide2, ref, wide1))
    second = run(plan2, 0)

    @pl.when(is_proj)
    def _():
        for copy in run(copies(True), 2):
            copy.wait()

    @pl.when(jnp.logical_not(is_proj))
    def _():
        for copy in run(copies(False), 2):
            copy.wait()

    for copy in second:
        copy.wait()


def weight_share(rank, core, qkv_weight, proj_weight, fc1_weight, ranks, block, unit):
    rows = qkv_weight.shape[0]
    wide1, wide2 = 2 * D // ranks, fc1_weight.shape[1] // 2 // ranks
    out = jax.ShapeDtypeStruct((rows, wide1 + wide2), bf16)
    return pl.pallas_call(
        functools.partial(share_kernel, (wide1, wide2, block, unit, D // 2)),
        out_shape=[out, out],
        grid_spec=pltpu.PrefetchScalarGridSpec(
            num_scalar_prefetch=1,
            grid=(1,),
            in_specs=[pl.BlockSpec(memory_space=pl.ANY)] * 3,
            out_specs=[pl.BlockSpec(out.shape, lambda i, a: (0, 0))] * 2,
            scratch_shapes=[pltpu.SemaphoreType.DMA((2 + 2 * (wide1 // block),))],
        ),
        cost_estimate=SHORT,
        name="weight_share",
    )(jnp.stack([rank, core]).astype(jnp.int32), qkv_weight, proj_weight, fc1_weight)


def whole_specs(arrays):
    return [pl.BlockSpec(a.shape, lambda *_, n=len(a.shape): (0,) * n) for a in arrays]


def slot_lists(sizes):
    slots = []
    for number, size in enumerate(sizes):
        for start in range(0, size, LANES):
            slots.append((number, start, min(LANES, size - start)))
    return slots


def pack_kernel(slots, *refs):
    *sources, out_ref, held = refs
    per_row = held.shape[1] // LANES
    held[...] = jnp.zeros_like(held)
    for slot, (number, start, size) in enumerate(slots):
        row, at = slot // per_row, slot % per_row * LANES
        held[row : row + 1, at : at + size] = sources[number][:, start : start + size].astype(f32)
    out_ref[...] = held[...].astype(out_ref.dtype)


def pack_small(vectors, width, slots):
    shape = (32 * LANES // width, width)
    vectors = [v.reshape(1, -1) for v in vectors]
    return pl.pallas_call(
        functools.partial(pack_kernel, slots),
        out_shape=jax.ShapeDtypeStruct(shape, bf16),
        scratch_shapes=[pltpu.VMEM(shape, f32)],
        name="pack_small",
    )(*vectors)


def unpack_kernel(slots, depth, index_ref, *refs):
    pieces, (vec_ref, unit_ref, tag_ref) = refs[:depth], refs[depth:]
    here, core = index_ref[0], index_ref[1]
    rows, width = pieces[0].shape
    per_row = width // LANES
    single = sum(1 for number, _, _ in slots if number < 10)
    vec_ref[...] = jnp.zeros_like(vec_ref)
    for k in range(depth):
        place = lax.rem(here - k + depth, depth)
        values = pieces[k][...].astype(f32)

        def part(side, slot, size):
            row, at = side * (rows // 2) + slot // per_row, slot % per_row * LANES
            return values[row : row + 1, at : at + size]

        for slot, (number, start, size) in enumerate(slots):
            own, other = part(0, slot, size), part(1, slot, size)
            first = jnp.where(core == 0, own, other)
            second = jnp.where(core == 0, other, own)
            if number < 10:
                at = pl.multiple_of(place * 2 * size, 2 * size)
                vec_ref[number : number + 1, pl.ds(at, 2 * size)] = jnp.concatenate([first, second], axis=1)
            elif number == 10:
                wide = unit_ref.shape[1] // depth
                unit_ref[0:1, pl.ds(pl.multiple_of(place * wide + start, LANES), LANES)] = own
            else:
                wide = tag_ref.shape[1] // depth
                at = pl.multiple_of(place * wide + start, LANES)
                tag_ref[0:1, pl.ds(at, LANES)] = first
                tag_ref[0:1, pl.ds(pl.multiple_of(at + wide // 2, LANES), LANES)] = second


def unpack_small(pieces, slots, rows, here, core, units, group_tokens):
    depth = len(pieces)
    extra, width = pieces[0].shape[0] - rows, pieces[0].shape[1]
    shapes = [(16, D), (1, units), (1, group_tokens)]
    return pl.pallas_call(
        functools.partial(unpack_kernel, slots, depth),
        out_shape=[jax.ShapeDtypeStruct(s, f32) for s in shapes],
        grid_spec=pltpu.PrefetchScalarGridSpec(
            num_scalar_prefetch=1,
            grid=(1,),
            in_specs=[pl.BlockSpec((extra, width), lambda i, a: (rows // extra, 0))] * depth,
            out_specs=[pl.BlockSpec(s, lambda i, a: (0, 0)) for s in shapes],
        ),
        name="unpack_small",
    )(jnp.stack([here, core]).astype(jnp.int32), *pieces)


def pack_grads_kernel(depth, sizes, index_ref, *refs):
    *sources, out_ref = refs
    core = index_ref[0]
    out_ref[...] = jnp.zeros_like(out_ref)
    for z in range(depth):
        for c in range(2):
            row = 16 * c
            for source, (size, of_core) in zip(sources, sizes):
                for start in range(0, size, LANES):
                    lanes = min(LANES, size - start)
                    at = (z if of_core else 2 * z + c) * size + start
                    value = source[0:1, at : at + lanes]
                    if of_core:
                        value = jnp.where(core == c, value, 0.0)
                    out_ref[z, row : row + 1, 0:lanes] = value
                    row += 1


def pack_grads(vectors, sizes, core, depth):
    return pl.pallas_call(
        functools.partial(pack_grads_kernel, depth, sizes),
        out_shape=jax.ShapeDtypeStruct((depth, 32, LANES), f32),
        grid_spec=pltpu.PrefetchScalarGridSpec(
            num_scalar_prefetch=1,
            grid=(1,),
            in_specs=whole_specs(vectors),
            out_specs=pl.BlockSpec((depth, 32, LANES), lambda i, a: (0, 0, 0)),
        ),
        name="pack_grads",
    )(core.reshape(1).astype(jnp.int32), *vectors)


def grad_blocks_kernel(orders, ranks, index_ref, a_ref, b_ref, *refs):
    outs, held = refs[:-1], refs[-1]
    rank = index_ref[0]
    held[...] = dot_tn(a_ref[...], b_ref[...]).astype(bf16)
    width = held.shape[1] // ranks
    share = held.shape[0] // len(orders)
    for n, order in enumerate(orders):
        for which, offsets in enumerate(halves(ranks, order[0], list(range(ranks)))):
            for i, o in enumerate(offsets):
                cols = pl.ds(pl.multiple_of((rank ^ o) * width, width), width)
                outs[2 * n + which][i, 0] = held[n * share : (n + 1) * share, cols]


def grad_blocks(a, b, rank, orders, name):
    depth, ranks = lax.axis_size("fsdp") // 2, lax.axis_size("rep")
    tokens, rows, cols = a.shape[0], a.shape[1] // depth, b.shape[1]
    if cols // ranks % LANES:
        return relative_blocks(dot_tn(a, b).astype(bf16), rank, orders)
    block = (ranks // 2, depth, rows // len(orders), cols // ranks)
    outs = pl.pallas_call(
        functools.partial(grad_blocks_kernel, orders, ranks),
        out_shape=[jax.ShapeDtypeStruct(block, bf16)] * (2 * len(orders)),
        grid_spec=pltpu.PrefetchScalarGridSpec(
            num_scalar_prefetch=1,
            grid=(depth,),
            in_specs=[
                pl.BlockSpec((tokens, rows), lambda i, s: (0, i)),
                pl.BlockSpec((tokens, cols), lambda i, s: (0, 0)),
            ],
            out_specs=[pl.BlockSpec((block[0], 1) + block[2:], lambda i, s: (0, i, 0, 0))] * (2 * len(orders)),
            scratch_shapes=[pltpu.VMEM((rows, cols), bf16)],
        ),
        compiler_params=pltpu.CompilerParams(vmem_limit_bytes=40 << 20),
        cost_estimate=SHORT,
        name=name,
    )(rank.reshape(1).astype(jnp.int32), a, b)
    return [(outs[2 * n], outs[2 * n + 1]) for n in range(len(orders))]


def pre_grad_kernel(g_ref, w_ref, slope_ref, out_ref, sum_ref):
    grad = dot_nt(g_ref[...], w_ref[...]) * slope_ref[...].astype(f32)
    out_ref[...] = grad.astype(bf16)
    sum_ref[...] = jnp.sum(grad, axis=0, keepdims=True)


def pre_grads(mlp_grad, fc2_matrix, slope):
    tokens, units = slope.shape
    tile = 256
    return pl.pallas_call(
        pre_grad_kernel,
        out_shape=[jax.ShapeDtypeStruct((tokens, units), bf16), jax.ShapeDtypeStruct((1, units), f32)],
        grid=(units // tile,),
        in_specs=[
            pl.BlockSpec((tokens, D), lambda i: (0, 0)),
            pl.BlockSpec((tile, D), lambda i: (i, 0)),
            pl.BlockSpec((tokens, tile), lambda i: (0, i)),
        ],
        out_specs=[pl.BlockSpec((tokens, tile), lambda i: (0, i)), pl.BlockSpec((1, tile), lambda i: (0, i))],
        compiler_params=pltpu.CompilerParams(vmem_limit_bytes=40 << 20),
        cost_estimate=SHORT,
        name="pre_grad",
    )(mlp_grad, fc2_matrix, slope)


def product_kernel(half_ref, first_ref, second_ref, w_ref, out1_ref, out2_ref):
    out1_ref[...] = dot(first_ref[...], w_ref[...])
    out2_ref[...] = dot(second_ref[...], w_ref[...])


def product_nt_kernel(half_ref, first_ref, second_ref, w_ref, out1_ref, out2_ref, held):
    @pl.when(pl.program_id(0) == 0)
    def _():
        held[...] = w_ref[...].T

    out1_ref[...] = dot(first_ref[...], held[...])
    out2_ref[...] = dot(second_ref[...], held[...])


def product(a, weight, flipped, half, name):
    rows, tile = a.shape[0] // 2, 128
    count = rows // tile
    out = pl.BlockSpec((tile, D), lambda i, h: (i, 0))
    return pl.pallas_call(
        product_nt_kernel if flipped else product_kernel,
        out_shape=[jax.ShapeDtypeStruct((rows, D), f32)] * 2,
        grid_spec=pltpu.PrefetchScalarGridSpec(
            num_scalar_prefetch=1,
            grid=(count,),
            in_specs=[
                pl.BlockSpec((tile, a.shape[1]), lambda i, h: (i + h[0] * count, 0)),
                pl.BlockSpec((tile, a.shape[1]), lambda i, h: (i + (1 - h[0]) * count, 0)),
                pl.BlockSpec(weight.shape, lambda i, h: (0, 0)),
            ],
            out_specs=[out, out],
            scratch_shapes=[pltpu.VMEM(weight.shape[::-1], bf16)] if flipped else [],
        ),
        compiler_params=pltpu.CompilerParams(vmem_limit_bytes=32 << 20),
        cost_estimate=SHORT,
        name=name,
    )(jnp.asarray(half, jnp.int32).reshape(1), a, a, weight)


def finish_kernel(
    own1_ref, sent1_ref, tok_ref, grad_ref, own2_ref, sent2_ref, resid_ref, cot_ref, vec_ref,
    in_grad_ref, out_ref, sum_ref,
):
    grad = own1_ref[...] + sent1_ref[...]
    normal, inverse = normalize(tok_ref[...].astype(f32))
    in_grad_ref[...] = grad_ref[...] + norm_back(grad, normal, inverse, vec_ref[0:1, :])
    mlp = own2_ref[...] + sent2_ref[...] + vec_ref[8:9, :]
    out_ref[...] = (resid_ref[...] + vec_ref[9:10, :] * mlp).astype(bf16)
    out_grad = cot_ref[...].astype(f32)

    @pl.when(pl.program_id(0) == 0)
    def _():
        sum_ref[...] = jnp.zeros_like(sum_ref)

    for row, value in enumerate((grad * normal, grad, out_grad * vec_ref[9:10, :], out_grad * mlp)):
        sum_ref[row : row + 1, :] += jnp.sum(value, axis=0, keepdims=True)


def finish(own1, sent1, tok, resid_grad, own2, sent2, resid, cot, vecs):
    rows, tile = own1.shape[0], 64
    part = pl.BlockSpec((tile, D), lambda i: (i, 0))
    return pl.pallas_call(
        finish_kernel,
        out_shape=[
            jax.ShapeDtypeStruct((rows, D), f32), jax.ShapeDtypeStruct((rows, D), bf16),
            jax.ShapeDtypeStruct((8, D), f32),
        ],
        grid=(rows // tile,),
        in_specs=[part] * 8 + [pl.BlockSpec(vecs.shape, lambda i: (0, 0))],
        out_specs=[part, part, pl.BlockSpec((8, D), lambda i: (0, 0))],
        compiler_params=pltpu.CompilerParams(vmem_limit_bytes=24 << 20),
        cost_estimate=SHORT,
        name="finish",
    )(own1, sent1, tok, resid_grad, own2, sent2, resid, cot, vecs)


def residual_kernel(own_ref, sent_ref, tok_ref, vec_ref, attn_ref, resid_ref, input_ref):
    attn = own_ref[...] + sent_ref[...] + vec_ref[4:5, :]
    resid = tok_ref[...].astype(f32) + vec_ref[5:6, :] * attn
    attn_ref[...] = attn
    resid_ref[...] = resid
    normal, _ = normalize(resid)
    input_ref[...] = (normal * vec_ref[6:7, :] + vec_ref[7:8, :]).astype(bf16)


def residual(own, sent, tok, vecs):
    rows, tile = own.shape[0], 64
    part = pl.BlockSpec((tile, D), lambda i: (i, 0))
    return pl.pallas_call(
        residual_kernel,
        out_shape=[jax.ShapeDtypeStruct((rows, D), t) for t in (f32, f32, bf16)],
        grid=(rows // tile,),
        in_specs=[part] * 3 + [pl.BlockSpec(vecs.shape, lambda i: (0, 0))],
        out_specs=[part] * 3,
        compiler_params=pltpu.CompilerParams(vmem_limit_bytes=24 << 20),
        cost_estimate=SHORT,
        name="residual",
    )(own, sent, tok, vecs)


def scaled_kernel(own_ref, other_ref, vec_ref, out_ref):
    rows = own_ref.shape[0]
    for n, ref in enumerate((own_ref, other_ref)):
        out_ref[n * rows : (n + 1) * rows, :] = (ref[...].astype(f32) * vec_ref[9:10, :]).astype(bf16)


def scaled(own, other, vecs):
    return pl.pallas_call(
        scaled_kernel,
        out_shape=jax.ShapeDtypeStruct((2 * own.shape[0], D), bf16),
        compiler_params=pltpu.CompilerParams(vmem_limit_bytes=24 << 20),
        cost_estimate=SHORT,
        name="scaled",
    )(own, other, vecs)


def units_kernel(n_ref, w_ref, b_ref, act_ref, slope_ref):
    act, slope = gelu_pair(dot(n_ref[...], w_ref[...]) + b_ref[...])
    act_ref[...] = act.astype(bf16)
    slope_ref[...] = slope.astype(bf16)


def hidden_units(normed, weight, bias):
    tokens, units = normed.shape[0], weight.shape[1]
    tile = 256
    part = pl.BlockSpec((tokens, tile), lambda i: (0, i))
    return pl.pallas_call(
        units_kernel,
        out_shape=[jax.ShapeDtypeStruct((tokens, units), bf16)] * 2,
        grid=(units // tile,),
        in_specs=[
            pl.BlockSpec((tokens, D), lambda i: (0, 0)),
            pl.BlockSpec((D, tile), lambda i: (0, i)),
            pl.BlockSpec((1, tile), lambda i: (0, i)),
        ],
        out_specs=[part, part],
        compiler_params=pltpu.CompilerParams(vmem_limit_bytes=32 << 20),
        cost_estimate=SHORT,
        name="units",
    )(normed, weight, bias)


def norm_grad_kernel(own_ref, sent_ref, resid_ref, cot_ref, attn_ref, vec_ref, grad_ref, scaled_ref, sum_ref):
    grad = own_ref[...] + sent_ref[...]
    normal, inverse = normalize(resid_ref[...])
    resid_grad = cot_ref[...].astype(f32) + norm_back(grad, normal, inverse, vec_ref[6:7, :])
    scaled = resid_grad * vec_ref[5:6, :]
    grad_ref[...] = resid_grad
    scaled_ref[...] = scaled.astype(bf16)

    @pl.when(pl.program_id(0) == 0)
    def _():
        sum_ref[...] = jnp.zeros_like(sum_ref)

    for row, value in enumerate((grad * normal, grad, scaled, resid_grad * attn_ref[...])):
        sum_ref[row : row + 1, :] += jnp.sum(value, axis=0, keepdims=True)


def norm_grads(own, sent, resid, cot, attn_out, vecs):
    rows, tile = own.shape[0], 64
    part = pl.BlockSpec((tile, D), lambda i: (i, 0))
    return pl.pallas_call(
        norm_grad_kernel,
        out_shape=[
            jax.ShapeDtypeStruct((rows, D), f32), jax.ShapeDtypeStruct((rows, D), bf16),
            jax.ShapeDtypeStruct((8, D), f32),
        ],
        grid=(rows // tile,),
        in_specs=[part] * 5 + [pl.BlockSpec(vecs.shape, lambda i: (0, 0))],
        out_specs=[part, part, pl.BlockSpec((8, D), lambda i: (0, 0))],
        compiler_params=pltpu.CompilerParams(vmem_limit_bytes=24 << 20),
        cost_estimate=SHORT,
        name="norm_grad",
    )(own, sent, resid, cot, attn_out, vecs)


def proj_grad_kernel(head_rows, c_ref, g_ref, out_ref):
    wide = out_ref.shape[1]
    for side in range(2):
        grad = dot_tn(c_ref[...], g_ref[:, side * wide : (side + 1) * wide]).astype(bf16)
        for z in range(grad.shape[0] // head_rows):
            at = (2 * z + side) * head_rows
            out_ref[at : at + head_rows, :] = grad[z * head_rows : (z + 1) * head_rows]


def packed_proj_grad(context, attn_grad, head_rows):
    wide = D // 2
    return pl.pallas_call(
        functools.partial(proj_grad_kernel, head_rows),
        out_shape=jax.ShapeDtypeStruct((D, wide), bf16),
        compiler_params=pltpu.CompilerParams(vmem_limit_bytes=32 << 20),
        cost_estimate=SHORT,
        name="proj_grad",
    )(context, attn_grad)


def qkv_grad_kernel(orders, ranks, depth, per, index_ref, n_ref, *refs):
    grads, p_ref = refs[: 3 * per], refs[3 * per]
    outs, held = refs[3 * per + 1 : -1], refs[-1]
    rank = index_ref[0]
    normed = n_ref[...]
    for number in range(3):
        pieces = [g[...] for g in grads[number * per : (number + 1) * per]]
        wide = per * LANES
        joined = pieces[0] if per == 1 else jnp.concatenate(pieces, axis=1)
        held[:, number * wide : (number + 1) * wide] = dot_tn(normed, joined).astype(bf16)
    held[:, 3 * per * LANES :] = p_ref[...]
    width = held.shape[1] // ranks
    rows = held.shape[0] // depth
    share = rows // len(orders)
    for n, order in enumerate(orders):
        for which, offsets in enumerate(halves(ranks, order[0], list(range(ranks)))):
            for i, o in enumerate(offsets):
                cols = pl.ds(pl.multiple_of((rank ^ o) * width, width), width)
                for z in range(depth):
                    at = z * rows + n * share
                    outs[2 * n + which][i, z] = held[at : at + share, cols]


def qkv_grad_blocks(normed, grads, proj_packed, part, parts, rank, orders):
    depth, ranks = lax.axis_size("fsdp") // 2, lax.axis_size("rep")
    per = len(grads) // 3
    cols = 4 * per * LANES
    block = (ranks // 2, depth, D // depth // len(orders), cols // ranks)
    tokens = normed.shape[0] // 3
    outs = pl.pallas_call(
        functools.partial(qkv_grad_kernel, orders, ranks, depth, per),
        out_shape=[jax.ShapeDtypeStruct(block, bf16)] * (2 * len(orders)),
        grid_spec=pltpu.PrefetchScalarGridSpec(
            num_scalar_prefetch=1,
            grid=(1,),
            in_specs=[pl.BlockSpec((tokens, D), lambda i, a: (1, 0))]
            + whole_specs(grads)
            + [pl.BlockSpec((D, per * LANES), lambda i, a: (0, part))],
            out_specs=[pl.BlockSpec(block, lambda i, a: (0, 0, 0, 0))] * (2 * len(orders)),
            scratch_shapes=[pltpu.VMEM((D, cols), bf16)],
        ),
        compiler_params=pltpu.CompilerParams(vmem_limit_bytes=40 << 20),
        cost_estimate=SHORT,
        name="qkv_grad",
    )(rank.reshape(1).astype(jnp.int32), normed, *grads, proj_packed)
    return [(outs[2 * n], outs[2 * n + 1]) for n in range(len(orders))]


def spread_lanes(tags, width):
    return jnp.concatenate([tags] * (width // LANES), axis=1)


def project_kernel(need_ref, n_ref, w_ref, b_ref, q_ref, k_ref, v_ref):
    row = pl.program_id(0)
    wide = q_ref.shape[1]

    @pl.when(need_ref[row] > 0)
    def _():
        n = n_ref[...]
        for i, ref in enumerate((q_ref, k_ref, v_ref)):
            out = dot(n, w_ref[:, i * wide : (i + 1) * wide]) + b_ref[0:1, i * wide : (i + 1) * wide]
            if i == 0:
                out = out.astype(bf16).astype(f32) * HEAD_DIM ** (-0.5)
            ref[...] = out.astype(bf16)

    @pl.when(need_ref[row] == 0)
    def _():
        for ref in (q_ref, k_ref, v_ref):
            ref[...] = jnp.zeros_like(ref)


def project(need, normed, weight, bias, wide):
    rows = normed.shape[0]
    return pl.pallas_call(
        project_kernel,
        out_shape=[jax.ShapeDtypeStruct((rows, wide), bf16)] * 3,
        grid_spec=pltpu.PrefetchScalarGridSpec(
            num_scalar_prefetch=1,
            grid=(rows // BLOCK,),
            in_specs=[
                pl.BlockSpec((BLOCK, D), lambda i, s: (i, 0)),
                pl.BlockSpec(weight.shape, lambda i, s: (0, 0)),
                pl.BlockSpec((1, 3 * wide), lambda i, s: (0, 0)),
            ],
            out_specs=[pl.BlockSpec((BLOCK, wide), lambda i, s: (i, 0))] * 3,
        ),
        compiler_params=pltpu.CompilerParams(vmem_limit_bytes=32 << 20),
        cost_estimate=SHORT,
        name="project",
    )(need, normed, weight, bias)


def norm_kernel(need_ref, info_ref, *refs):
    *sources, vec_ref, out_ref = refs
    row = pl.program_id(0)
    side = (row // info_ref[1]) % 2
    chip = row // (2 * info_ref[1])

    @pl.when(need_ref[row] > 0)
    def _():
        picked = jnp.where(chip == 0, sources[0][...], jnp.where(chip == 1, sources[2][...], sources[4][...]))
        theirs = jnp.where(chip == 0, sources[1][...], jnp.where(chip == 1, sources[3][...], sources[5][...]))
        picked = jnp.where(side == info_ref[0], picked, theirs)
        normal, _ = normalize(picked.astype(f32))
        out_ref[...] = (normal * vec_ref[0:1, :] + vec_ref[1:2, :]).astype(bf16)

    @pl.when(need_ref[row] == 0)
    def _():
        out_ref[...] = jnp.zeros_like(out_ref)


def norm_window(need, info, sources, vecs, window, count):
    per = count // BLOCK

    def spec(chip):
        def index(i, a, b):
            inside = jnp.clip(i - 2 * per * chip, 0, 2 * per - 1)
            return (inside % per, 0)

        return pl.BlockSpec((BLOCK, D), index)

    return pl.pallas_call(
        norm_kernel,
        out_shape=jax.ShapeDtypeStruct((window, D), bf16),
        grid_spec=pltpu.PrefetchScalarGridSpec(
            num_scalar_prefetch=2,
            grid=(window // BLOCK,),
            in_specs=[spec(i // 2) for i in range(6)] + [pl.BlockSpec(vecs.shape, lambda i, a, b: (0, 0))],
            out_specs=pl.BlockSpec((BLOCK, D), lambda i, a, b: (i, 0)),
        ),
        compiler_params=pltpu.CompilerParams(vmem_limit_bytes=24 << 20),
        cost_estimate=SHORT,
        name="norm_window",
    )(need, info, *sources, vecs)


def attend_kernel(lo_ref, hi_ref, first_ref, last_ref, q_ref, k_ref, v_ref, qt_ref, kt_ref, o_ref, lse_ref, s_ref, m_ref, acc_ref):
    i = pl.program_id(0)
    left = lax.broadcasted_iota(jnp.int32, (1, LANES), 1) < HEAD_DIM
    lo, hi = lo_ref[i], hi_ref[i]
    base = (first_ref.shape[0] - pl.num_programs(0)) // 2
    q = q_ref[...]
    zero = jnp.zeros_like(q)
    heads = (jnp.where(left, q, zero), jnp.where(left, zero, q))
    m_ref[...] = jnp.full_like(m_ref, MASKED)
    one_image = first_ref[base + i] == last_ref[base + i]
    folds = BLOCK // LANES

    def fold(value, combine):
        parts = [value[:, n * LANES : (n + 1) * LANES] for n in range(folds)]
        return functools.reduce(combine, parts)

    def scores(j, carry):
        at = pl.multiple_of(j * BLOCK, BLOCK)
        k = k_ref[pl.ds(at, BLOCK), :]
        inside = one_image & (first_ref[j] == first_ref[base + i]) & (last_ref[j] == first_ref[base + i])

        @pl.when(inside)
        def _():
            for h in range(2):
                s = dot_nt(heads[h], k)
                s_ref[h, j] = s
                m_ref[h] = jnp.maximum(m_ref[h], fold(s, jnp.maximum))

        @pl.when(jnp.logical_not(inside))
        def _():
            same = spread_lanes(qt_ref[...], BLOCK) == kt_ref[:, pl.ds(at, BLOCK)]
            for h in range(2):
                s = jnp.where(same, dot_nt(heads[h], k), MASKED)
                s_ref[h, j] = s
                m_ref[h] = jnp.maximum(m_ref[h], fold(s, jnp.maximum))

        return carry

    lax.fori_loop(lo, hi, scores, 0)
    tops = [jnp.max(m_ref[h], axis=1, keepdims=True) for h in range(2)]
    m_ref[...] = jnp.zeros_like(m_ref)
    acc_ref[...] = jnp.zeros_like(acc_ref)

    def mix(j, carry):
        at = pl.multiple_of(j * BLOCK, BLOCK)
        v = v_ref[pl.ds(at, BLOCK), :]
        for h in range(2):
            e = jnp.exp(s_ref[h, j] - tops[h])
            m_ref[h] += fold(e, jnp.add)
            acc_ref[h] += dot(e.astype(bf16), v)
        return carry

    lax.fori_loop(lo, hi, mix, 0)
    sums = [jnp.sum(m_ref[h], axis=1, keepdims=True) for h in range(2)]
    o_ref[...] = jnp.where(left, acc_ref[0] / sums[0], acc_ref[1] / sums[1]).astype(bf16)
    for h in range(2):
        lse = jnp.broadcast_to(tops[h] + jnp.log(sums[h]), (BLOCK, LANES))
        lse_ref[0, h : h + 1, :] = lse.T[0:1, :]


def attend(lo, hi, firsts, lasts, q, k, v, tag_cols, tag_row, own_rows, pair):
    window = q.shape[0]
    blocks = own_rows // BLOCK
    skip = (window - own_rows) // 2 // BLOCK
    return pl.pallas_call(
        attend_kernel,
        out_shape=[
            jax.ShapeDtypeStruct((own_rows, LANES), bf16),
            jax.ShapeDtypeStruct((1, 2, own_rows), f32),
        ],
        grid_spec=pltpu.PrefetchScalarGridSpec(
            num_scalar_prefetch=4,
            grid=(blocks,),
            in_specs=[
                pl.BlockSpec((BLOCK, LANES), lambda i, *_: (i + skip, pair)),
                pl.BlockSpec((window, LANES), lambda i, *_: (0, pair)),
                pl.BlockSpec((window, LANES), lambda i, *_: (0, pair)),
                pl.BlockSpec((BLOCK, LANES), lambda i, *_: (i + skip, 0)),
                pl.BlockSpec((1, window), lambda i, *_: (0, 0)),
            ],
            out_specs=[
                pl.BlockSpec((BLOCK, LANES), lambda i, *_: (i, 0)),
                pl.BlockSpec((1, 2, BLOCK), lambda i, *_: (0, 0, i)),
            ],
            scratch_shapes=[
                pltpu.VMEM((2, window // BLOCK, BLOCK, BLOCK), f32),
                pltpu.VMEM((2, BLOCK, LANES), f32),
                pltpu.VMEM((2, BLOCK, LANES), f32),
            ],
        ),
        compiler_params=pltpu.CompilerParams(vmem_limit_bytes=32 << 20),
        cost_estimate=SHORT,
        name="attend",
    )(lo, hi, firsts, lasts, q, k, v, tag_cols, tag_row)


def attend_back_kernel(
    start, stop, lo_ref, hi_ref, q_ref, k_ref, v_ref, g_ref, tc_ref, tr_ref, lse_ref, delta_ref,
    dq_ref, dk_ref, dv_ref, sum_ref, dk_acc, dv_acc, dq_acc,
):
    first = lax.broadcasted_iota(jnp.int32, (1, LANES), 1) < HEAD_DIM
    dk_acc[...] = jnp.zeros_like(dk_acc)
    dv_acc[...] = jnp.zeros_like(dv_acc)
    sum_ref[...] = jnp.zeros_like(sum_ref)

    def split(value):
        zero = jnp.zeros_like(value)
        return jnp.where(first, value, zero), jnp.where(first, zero, value)

    def visit(i, j, qs, gs, of_key, of_query):
        at_q, at_k = pl.multiple_of(i * BLOCK, BLOCK), pl.multiple_of(j * BLOCK, BLOCK)
        k = k_ref[pl.ds(at_k, BLOCK), :]
        v = v_ref[pl.ds(at_k, BLOCK), :]
        same = spread_lanes(tc_ref[pl.ds(at_k, BLOCK), :], BLOCK) == tr_ref[:, pl.ds(at_q, BLOCK)]
        ps, ds = [], []
        for h in range(2):
            s = dot_nt(k, qs[h])
            dp = dot_nt(v, gs[h])
            p = jnp.where(same, jnp.exp(s - lse_ref[0, h : h + 1, pl.ds(at_q, BLOCK)]), 0.0)
            d = p * (dp - delta_ref[0, h : h + 1, pl.ds(at_q, BLOCK)])
            ps.append(p.astype(bf16))
            ds.append(d.astype(bf16))
        if of_key:
            at = pl.multiple_of((j - start) * BLOCK, BLOCK)
            dv_acc[pl.ds(at, BLOCK), :] += dot(ps[0], gs[0]) + dot(ps[1], gs[1])
            dk_acc[pl.ds(at, BLOCK), :] += dot(ds[0], qs[0]) + dot(ds[1], qs[1])
        if of_query:
            ks = split(k)
            dq_acc[...] += dot_tn(ds[0], ks[0]) + dot_tn(ds[1], ks[1])

    def query_block(own_q, i, carry):
        at_q = pl.multiple_of(i * BLOCK, BLOCK)
        qs = split(q_ref[pl.ds(at_q, BLOCK), :])
        gs = split(g_ref[pl.ds(at_q, BLOCK), :])
        lo, hi = lo_ref[i], hi_ref[i]

        def keys(first_key, last_key, of_key):
            def body(j, carry):
                visit(i, j, qs, gs, of_key, own_q)
                return carry

            lax.fori_loop(first_key, last_key, body, 0)

        if own_q:
            dq_acc[...] = jnp.zeros_like(dq_acc)
            keys(lo, jnp.minimum(hi, start), False)
            keys(jnp.maximum(lo, stop), hi, False)
        keys(jnp.maximum(lo, start), jnp.minimum(hi, stop), True)
        if own_q:
            at = pl.multiple_of((i - start) * BLOCK, BLOCK)
            dq = dq_acc[...] * HEAD_DIM ** (-0.5)
            dq_ref[pl.ds(at, BLOCK), :] = dq.astype(bf16)
            sum_ref[0, 0:1, :] += jnp.sum(dq, axis=0, keepdims=True)
        return carry

    before = jnp.where(lo_ref[start] < start, lo_ref[start], start)
    after = jnp.maximum(hi_ref[stop - 1], stop)
    lax.fori_loop(before, start, functools.partial(query_block, False), 0)
    lax.fori_loop(start, stop, functools.partial(query_block, True), 0)
    lax.fori_loop(stop, after, functools.partial(query_block, False), 0)
    dk_ref[...] = dk_acc[...].astype(bf16)
    dv_ref[...] = dv_acc[...].astype(bf16)
    sum_ref[0, 1:2, :] = jnp.sum(dv_acc[...], axis=0, keepdims=True)


def attend_back(lo, hi, q, k, v, g, tag_cols, tag_row, lse, delta, own_rows, pair):
    window = q.shape[0]
    pairs, wide = 1, LANES
    grad_pair = pair % (g.shape[1] // LANES)
    start = (window - own_rows) // 2 // BLOCK
    stop = start + own_rows // BLOCK
    whole = lambda: pl.BlockSpec((window, LANES), lambda p, a, b: (0, pair))
    own = lambda: pl.BlockSpec((own_rows, LANES), lambda p, a, b: (0, p))
    stat = lambda: pl.BlockSpec((1, 2, window), lambda p, a, b: (pair, 0, 0))
    return pl.pallas_call(
        functools.partial(attend_back_kernel, start, stop),
        out_shape=[jax.ShapeDtypeStruct((own_rows, wide), bf16)] * 3
        + [jax.ShapeDtypeStruct((pairs, 8, LANES), f32)],
        grid_spec=pltpu.PrefetchScalarGridSpec(
            num_scalar_prefetch=2,
            grid=(pairs,),
            in_specs=[
                whole(), whole(), whole(),
                pl.BlockSpec((window, LANES), lambda p, a, b: (0, grad_pair)),
                pl.BlockSpec((window, LANES), lambda p, a, b: (0, 0)),
                pl.BlockSpec((1, window), lambda p, a, b: (0, 0)),
                stat(), stat(),
            ],
            out_specs=[own(), own(), own(), pl.BlockSpec((1, 8, LANES), lambda p, a, b: (p, 0, 0))],
            scratch_shapes=[
                pltpu.VMEM((own_rows, LANES), f32),
                pltpu.VMEM((own_rows, LANES), f32),
                pltpu.VMEM((BLOCK, LANES), f32),
            ],
        ),
        compiler_params=pltpu.CompilerParams(vmem_limit_bytes=40 << 20),
        cost_estimate=SHORT,
        name="attend_back",
    )(lo, hi, q, k, v, g, tag_cols, tag_row, lse, delta)


def on_device(
    tokens, image_ids, ln1_gain, ln1_bias, qkv_weight, query_bias, value_bias, proj_weight,
    proj_bias, scale_attn, ln2_gain, ln2_bias, fc1_weight, fc1_bias, fc2_weight, fc2_bias,
    scale_mlp, cotangent,
):
    devices = lax.axis_size("fsdp")
    depth, ranks = devices // 2, lax.axis_size("rep")
    place = lax.axis_index("fsdp")
    rank = lax.axis_index("rep")
    here, core = place // 2, place % 2
    count = tokens.shape[1]
    chip = 2 * count
    head_rows = D // devices
    ff = fc1_weight.shape[1]
    unit_rows = ff // devices
    half_heads = D // 2
    local_heads = half_heads // HEAD_DIM
    pairs = half_heads // LANES
    bits = list(range(rep_bits()))

    def in_order(own, other, axis=0):
        return jnp.where(
            core == 0,
            jnp.concatenate([own, other], axis=axis),
            jnp.concatenate([other, own], axis=axis),
        )

    def mine(value):
        return lax.dynamic_slice_in_dim(value, core * count, count, 0)

    def others(value):
        return lax.dynamic_slice_in_dim(value, (1 - core) * count, count, 0)

    def every_other(value, width, start):
        cuts = range(start * width, value.shape[1], 2 * width)
        return jnp.concatenate([value[:, c : c + width] for c in cuts], axis=1)

    def all_share(which):
        pick_cols = lambda v, w: jnp.where(which == 0, every_other(v, w, 0), every_other(v, w, 1))
        heads = lax.dynamic_slice_in_dim(
            jnp.concatenate(
                [
                    pick_cols(qkv_weight, head_rows),
                    lax.dynamic_slice_in_dim(proj_weight, which * half_heads, half_heads, 1),
                ],
                axis=1,
            ),
            rank * (2 * D // ranks), 2 * D // ranks, 1,
        )
        units = lax.dynamic_slice_in_dim(
            pick_cols(fc1_weight, unit_rows), rank * (ff // 2 // ranks), ff // 2 // ranks, 1
        )
        return jnp.concatenate([heads, units], axis=1)

    if head_rows % LANES:
        kept, given = all_share(core), all_share(1 - core)
    else:
        kept, given = weight_share(
            rank, core, qkv_weight, proj_weight, fc1_weight, ranks, head_rows, unit_rows
        )
    wide1 = 2 * D // ranks
    got = swap_cores(given)
    is_proj = rank * wide1 >= 3 * half_heads
    own1 = in_order(kept[:, :wide1], jnp.where(is_proj, given[:, :wide1], got[:, :wide1]))
    own2 = in_order(kept[:, wide1:], got[:, wide1:])
    own3 = lax.dynamic_slice_in_dim(fc2_weight, rank * (D // ranks), D // ranks, 1)
    small = (
        ln1_gain, ln1_bias, query_bias, value_bias, proj_bias, scale_attn, ln2_gain, ln2_bias,
        fc2_bias, scale_mlp, fc1_bias, (image_ids[0] + 1).astype(bf16),
    )
    sizes = [v.shape[0] for v in small]
    slots = slot_lists(sizes)
    width = 2 * D // ranks
    small = pack_small(small, width, slots)
    small_other = swap_cores(small)
    rows1, rows3 = own1.shape[0], own3.shape[0]
    tok, cot = tokens[0], cotangent[0]
    tok_other = swap_cores(tok)
    cot_other = swap_cores(cot)
    own1 = jnp.concatenate([own1, small, small_other])
    own1, own2, own3, tok = tie(own1, own2, own3, tok)
    pieces1 = fetch_z(own1)
    tok, pieces1[1] = tie(tok, pieces1[1])
    behind, ahead = from_chip(tok, 1), from_chip(tok, -1)
    gather1 = Gather(pieces1, rows1, "gather1")
    gather1.send()
    behind_other, ahead_other = swap_cores(behind), swap_cores(ahead)
    for _ in bits[1:]:
        gather1.send()

    vec_rows, fc1_shift, all_tags = unpack_small(
        pieces1, slots, rows1, here, core, ff // 2, devices * count
    )
    vector = lambda i: vec_rows[i : i + 1]
    (
        attn_gain, attn_shift, query_shift, value_shift, proj_shift, attn_scale, mlp_gain,
        mlp_shift, fc2_shift, mlp_scale,
    ) = map(vector, range(10))
    core_part = lambda vec: jnp.where(
        core == 0, every_other(vec, head_rows, 0), every_other(vec, head_rows, 1)
    )

    window = 3 * chip
    padded = jnp.concatenate(
        [jnp.zeros((1, chip), f32), all_tags, jnp.full((1, chip), 1e6, f32)], axis=1
    )
    tag_row = lax.dynamic_slice(padded, (0, here * chip), (1, window))
    tags = tag_row.reshape(window)
    firsts, lasts = tags[::BLOCK], tags[BLOCK - 1 :: BLOCK]
    real = firsts * (1e6 - firsts) > 0
    below = jnp.sum((tag_row < firsts[:, None]).astype(jnp.int32), axis=1)
    upto = jnp.sum((tag_row <= lasts[:, None]).astype(jnp.int32), axis=1)
    blocks = window // BLOCK
    block_lo = jnp.where(real, below // BLOCK, 0)
    block_hi = jnp.where(real, (upto + BLOCK - 1) // BLOCK, 0)
    own_lo, own_hi = chip // BLOCK, 2 * chip // BLOCK
    numbers = jnp.arange(blocks)
    need = jnp.logical_and(numbers >= block_lo[own_lo], numbers < block_hi[own_hi - 1]).astype(jnp.int32)
    firsts, lasts = firsts.astype(jnp.int32), lasts.astype(jnp.int32)
    tag_cols = jnp.broadcast_to(tags[:, None], (window, LANES))

    info = jnp.stack([core, jnp.int32(count // BLOCK)]).astype(jnp.int32)
    normed1 = norm_window(
        need, info, (behind, behind_other, tok, tok_other, ahead, ahead_other), vec_rows, window, count
    )

    normed1, own2 = tie(normed1, own2)
    pieces2 = fetch_z(own2)
    normed1 = gather1.arrive(normed1)
    qkv_matrix, proj_matrix = gather1.assemble(here, rank, head_rows)

    shifts = jnp.concatenate(
        [core_part(query_shift), jnp.zeros((1, half_heads), f32), core_part(value_shift)], axis=1
    )
    queries, keys, values = project(need, normed1, qkv_matrix, shifts, half_heads)

    contexts, lses = [], []
    los = block_lo[own_lo:own_hi]
    los, queries = tie(los, queries)
    for pair in range(pairs):
        if pair == 1:
            los, own3, *pieces2 = tie(los, own3, *pieces2)
            gather2 = Gather(pieces2, rows1, "gather2")
            los = gather2.send(los)
            pieces3 = fetch_z(own3)
        if pair == 2:
            los = gather2.arrive(los)
            los = gather2.send(los)
        if pair == 3:
            los = gather2.arrive(los)
            for _ in bits[2:]:
                los = gather2.arrive(gather2.send(los))
            los, *pieces3 = tie(los, *pieces3)
            gather3 = Gather(pieces3, rows3, "gather3")
            los = gather3.send(los)
        context, lse = attend(
            los, block_hi[own_lo:own_hi], firsts, lasts, queries, keys, values, tag_cols,
            tag_row, chip, pair,
        )
        los, context = tie(los, context)
        contexts.append(context)
        lses.append(lse)
    context = jnp.concatenate(contexts, axis=1)
    lse_rows = jnp.concatenate(lses).reshape(local_heads, chip)
    context = gather3.arrive(context)
    context = gather3.send(context)
    own, given = product(context, proj_matrix, False, core, "attn_out")
    attn_out, resid, mlp_input = residual(own, swap_cores(given), tok, vec_rows)
    mlp_input = jnp.concatenate([mlp_input, swap_cores(mlp_input)])
    fc1_matrix = gather2.assemble(here, rank)
    activated, slope = hidden_units(mlp_input, fc1_matrix, fc1_shift)
    mlp_grad = scaled(cot, cot_other, vec_rows)
    both = [bits, bits[::-1]]
    activated = gather3.arrive(activated)
    for _ in bits[2:]:
        activated = gather3.arrive(gather3.send(activated))
    reduce3 = Reduce(grad_blocks(activated, mlp_grad, rank, both, "fc2_grad"), here, both)
    mlp_grad = reduce3.send(mlp_grad)
    fc2_matrix = gather3.assemble(here, rank)
    pre_grad, fc1_bias_part = pre_grads(mlp_grad, fc2_matrix, slope)
    reduce2 = Reduce(grad_blocks(mlp_input, pre_grad, rank, both, "fc1_grad"), here, both)
    pre_grad, _ = tie(pre_grad, [give for _, _, give in reduce2.held])
    own, given = product(pre_grad, fc1_matrix, True, 0, "mlp_in_grad")
    own, given = reduce3.arrive(own, given)
    for _ in bits[2:]:
        own, given = reduce3.arrive(*reduce3.send(own, given))
    own, given = reduce3.send(own, given)
    sent = swap_cores(given)
    resid_grad, attn_grad, norm_sums = norm_grads(own, sent, resid, cot, attn_out, vec_rows)
    both_grads = jnp.zeros((chip, D), bf16)
    for part, which in ((attn_grad, core), (swap_cores(attn_grad), 1 - core)):
        both_grads = lax.dynamic_update_slice_in_dim(both_grads, part, which * count, 0)
    attn_grad = both_grads
    context_grad = dot_nt(attn_grad, proj_matrix).astype(bf16)
    head_of = (
        lax.broadcasted_iota(jnp.int32, (local_heads, half_heads), 1) // HEAD_DIM
        == lax.broadcasted_iota(jnp.int32, (local_heads, half_heads), 0)
    ).astype(f32)
    row_delta = lax.dot_general(
        head_of, context_grad.astype(f32) * context.astype(f32), (((1,), (1,)), ((), ())),
        precision=lax.Precision.HIGHEST, preferred_element_type=f32,
    )
    stats = jnp.concatenate([lse_rows, row_delta])
    context_grad, activated, attn_grad = tie(context_grad, activated, attn_grad)
    chunk = half_heads // 2
    chunks = [context_grad[:, :chunk], context_grad[:, chunk:]]
    grads_behind, grads_ahead = zip(*[(from_chip(c, 1), from_chip(c, -1)) for c in chunks])
    stats_behind, stats_ahead = from_chip(stats, 1), from_chip(stats, -1)
    proj_grad = packed_proj_grad(context, attn_grad, head_rows)
    stat_window = jnp.concatenate([stats_behind, stats, stats_ahead], axis=1)
    by_pair = lambda s: s.reshape(pairs, 2, window)
    lse_window, delta_window = by_pair(stat_window[:local_heads]), by_pair(stat_window[local_heads:])

    half_pairs = pairs // 2
    half_width = half_heads // 2

    def first_group(parts, number):
        grads = [g for kind in zip(*parts) for g in kind]
        return Reduce(
            qkv_grad_blocks(normed1, grads, proj_grad, number, 2, rank, both), here, both
        )

    parts, sums = [], []
    out_own, out_given = product(activated, fc2_matrix, False, 0, "mlp_out")
    first, delta_window, lo, out_own, out_given = settle(
        ((grads_behind[0], grads_ahead[0]), delta_window, block_lo, out_own, out_given),
        (reduce3, "received"),
    )
    grad_windows = [jnp.concatenate([first[0], chunks[0], first[1]])]
    for pair in range(pairs):
        if pair == 0:
            lo = reduce3.arrive(lo)
            lo = reduce2.send(lo)
        if pair == 1:
            lo, second = settle((lo, (grads_behind[1], grads_ahead[1])), (reduce2, "received"))
            grad_windows.append(jnp.concatenate([second[0], chunks[1], second[1]]))
            lo = reduce2.arrive(lo)
            lo = reduce3.send_z(lo)
            for _ in bits[2:]:
                lo = reduce2.arrive(reduce2.send(lo))
            lo = reduce2.send(lo)
        if pair == 2:
            lo = settle(lo, (reduce2, "received"), (reduce3, "pieces"))
            lo = reduce2.arrive(lo)
            lo = reduce2.send_z(lo)
            reduce1a = first_group(parts, 0)
            lo = reduce1a.send(lo)
        if pair == 3:
            lo = settle(lo, (reduce2, "pieces"), (reduce1a, "received"))
            lo = reduce3.arrive_z(lo)
            lo = reduce2.arrive_z(lo)
            fc2_part = reduce3.total.astype(bf16)
            fc1_part = reduce2.total.astype(bf16)
            split = fc2_part.shape[0] // fc1_part.shape[0]
            mlp_spread = Spread(jnp.concatenate([fc1_part, *jnp.split(fc2_part, split)], axis=1))
            lo = mlp_spread.send(lo)
            lo = reduce1a.arrive(lo)
            for _ in bits[2:]:
                lo = reduce1a.arrive(reduce1a.send(lo))
            lo = reduce1a.send(lo)
        *grads, total = attend_back(
            lo, block_hi, queries, keys, values, grad_windows[pair * 2 // pairs], tag_cols, tag_row, lse_window,
            delta_window, chip, pair,
        )
        lo, *grads = tie(lo, *grads)
        parts.append(grads)
        sums.append(total[0])

    parts[-1] = settle(parts[-1], (mlp_spread, "arrays"))
    parts[-1] = reduce1a.arrive(parts[-1])
    parts[-1] = reduce1a.send_z(parts[-1])
    reduce1b = first_group(parts[half_pairs:], 1)
    parts[-1] = reduce1b.send(parts[-1])
    every = [jnp.concatenate(p, axis=1) for p in zip(*parts)]

    factor = 1.0 / math.sqrt(count * devices * ranks)
    in_own, in_given = product(
        jnp.concatenate(every, axis=1), qkv_matrix, True, core, "attn_in_grad"
    )
    tail = (in_own, in_given)
    tail = settle(tail, (reduce1b, "received"), (reduce1a, "pieces"))
    for _ in bits[1:]:
        tail = reduce1b.arrive(tail)
        tail = reduce1b.send(tail)
    in_own, in_given = tail
    input_rows, output_rows, end_sums = finish(
        in_own, swap_cores(in_given), tok, resid_grad, out_own, swap_cores(out_given), resid, cot, vec_rows
    )

    vectors = (
        end_sums[0:1], end_sums[1:2],
        jnp.concatenate([s[0:1] for s in sums], axis=1), jnp.concatenate([s[1:2] for s in sums], axis=1),
        norm_sums[2:3], norm_sums[3:4], norm_sums[0:1], norm_sums[1:2],
        end_sums[2:3], end_sums[3:4], fc1_bias_part,
    )
    of_core = [number in (2, 3, 10) for number in range(11)]
    partial = pack_grads(vectors, list(zip(sizes, of_core)), core, depth)
    vec_width = D // ranks
    half_of = lambda which: lax.dynamic_slice_in_dim(partial, which * 16, 16, 1)
    partial = half_of(core) + swap_cores(half_of(1 - core))
    vec_high = lax.reduce_precision(partial, 8, 7)
    side_by_side = 2 if vec_width >= 2 * LANES else 1
    extra = jnp.concatenate([vec_high, partial - vec_high], axis=side_by_side).astype(bf16)
    extra = jnp.pad(extra, ((0, 0), (0, 0), (0, vec_width - extra.shape[2])))
    extra = reduce1b.arrive(extra)
    extra = reduce1b.send_z(extra, extra=extra)
    for _ in bits[1:]:
        mlp_spread.send(extra)

    reduce1a.arrive_z()
    reduce1b.arrive_z()
    rows = reduce1a.total.shape[0]
    vec_total = reduce1b.total[rows:]
    if side_by_side == 2:
        vec_total = vec_total[:, :LANES] + vec_total[:, LANES : 2 * LANES]
    else:
        vec_total = vec_total[:16] + vec_total[16:]
    vec_high = lax.reduce_precision(vec_total, 8, 7)
    sides = [jnp.pad(v, ((0, 16), (0, vec_width - LANES))) for v in (vec_high, vec_total - vec_high)]
    payload = jnp.concatenate(
        [
            jnp.concatenate([reduce1a.total, reduce1b.total[:rows]], axis=1),
            jnp.concatenate(sides, axis=1),
        ]
    ).astype(bf16)
    payload = settle(payload, (mlp_spread, "arrays"))
    first_spread = Spread(payload)
    for bit in bits:
        first_spread.send()

    mlp_cols = fc1_part.shape[1]
    fc1_full = mlp_spread.blocks(rank, 0, mlp_cols)
    fc2_width = fc2_part.shape[1]
    fc2_full = tie(*[mlp_spread.blocks(rank, mlp_cols + n * fc2_width, fc2_width) for n in range(split)])
    grad_fc2 = jnp.concatenate(fc2_full).astype(f32) * factor
    first_a = first_spread.blocks(rank, 0, vec_width)
    first_b = first_spread.blocks(rank, vec_width, vec_width)
    totals = sum(
        part[rows : rows + 16, r * vec_width : r * vec_width + LANES].astype(f32)
        for part in (first_a, first_b)
        for r in range(ranks)
    ) * factor
    first_a, first_b = first_a[:rows], first_b[:rows]

    def rows_of(value, index):
        return lax.dynamic_slice_in_dim(value, index * head_rows, head_rows, 0)

    def interleave(own, other, width):
        cuts = range(0, own.shape[1], width)
        zipped = lambda a, b: jnp.concatenate(
            [v[:, c : c + width] for c in cuts for v in (a, b)], axis=1
        )
        return jnp.where(core == 0, zipped(own, other), zipped(other, own)).astype(f32) * factor

    fc1_other = swap_cores(rows_of(fc1_full, 1 - core))
    grad_fc1 = interleave(rows_of(fc1_full, core), fc1_other, unit_rows)
    qkv_full = jnp.concatenate(
        [
            part[:, n * half_width : (n + 1) * half_width]
            for n in range(3)
            for part in (first_a, first_b)
        ],
        axis=1,
    )
    grad_qkv = interleave(rows_of(qkv_full, core), swap_cores(rows_of(qkv_full, 1 - core)), head_rows)
    proj_part = jnp.concatenate([first_a[:, 3 * half_width :], first_b[:, 3 * half_width :]], axis=1)
    grad_proj = jnp.concatenate([proj_part[:head_rows], proj_part[head_rows:]], axis=1).astype(f32) * factor

    small_grads = [totals[i, : sizes[i]] for i in range(10)]
    lines = -(-sizes[10] // LANES)
    small_grads.append(totals[10 : 10 + lines].reshape(-1))
    (
        grad_attn_gain, grad_attn_shift, grad_query_shift, grad_value_shift, grad_proj_shift,
        grad_attn_scale, grad_mlp_gain, grad_mlp_shift, grad_fc2_shift, grad_mlp_scale, grad_fc1_shift,
    ) = small_grads

    return (
        output_rows[None],
        input_rows[None],
        grad_attn_gain,
        grad_attn_shift,
        grad_qkv,
        grad_query_shift,
        grad_value_shift,
        grad_proj,
        grad_proj_shift,
        grad_attn_scale,
        grad_mlp_gain,
        grad_mlp_shift,
        grad_fc1,
        grad_fc1_shift,
        grad_fc2,
        grad_fc2_shift,
        grad_mlp_scale,
    )


def solution(mesh):
    rows = P("fsdp", None)
    vec = P("fsdp")
    tok = P("rep", "fsdp", None)
    return jax.shard_map(
        on_device,
        mesh=mesh,
        in_specs=(
            tok, P("rep", "fsdp"), vec, vec, rows, vec, vec, rows, vec, vec, vec, vec, rows, vec,
            rows, vec, vec, tok,
        ),
        out_specs=(
            tok, tok, vec, vec, rows, vec, vec, rows, vec, vec, vec, vec, rows, vec, rows, vec, vec,
        ),
        check_vma=False,
    )
```

profile of v0, /device:TPU:0, one launch (start us, length us, event | category | flops | bytes accessed | tf_op | source)
XLA Modules:
  0.0 534.9 jit_solution(2298383754077751433)
XLA Ops:
  1.3 2.5 weight_share.1
  10.7 3.1 collective-permute-start.3
  13.8 2.6 collective-permute-start.4
  17.7 5.8 %collective-permute-done.3.refs_1_ = bf16[272,512]{1,0:T(8,128)(2,1)} collective-permute-done((bf16[272,512]{1,0:T(8,128)(2,1)S(1)}, bf16[272,512]{1,0:T(8,128)(2,1)}, u32[]{:S(2)}, u32[]{:S(2)}) %collective-permute-start.3) | collective-permute-done | bytes 278560 | tf_op jit(solution)/shard_map/ppermute | solution.py:66
  24.9 14.0 %collective-permute-start.6 = (bf16[512,1024]{1,0:T(8,128)(2,1)S(1)}, bf16[512,1024]{1,0:T(8,128)(2,1)}, u32[]{:S(2)}, u32[]{:S(2)}) collective-permute-start(bf16[512,1024]{1,0:T(8,128)(2,1)S(1)} %bitcast.262), channel_id=1, source_target_pairs={{0,2},{1,3},{2,4},{3,5},{4,6},{5,7},{8,10},{9,11},{10,12},{11,13},... | collective-permute-start | bytes 3145736 | tf_op jit(solution)/shard_map/ppermute | solution.py:72
  49.8 7.3 %collective-permute-done.9.refs_4_ = bf16[512,1024]{1,0:T(8,128)(2,1)S(1)} collective-permute-done((bf16[512,1024]{1,0:T(8,128)(2,1)S(1)}, bf16[512,1024]{1,0:T(8,128)(2,1)S(1)}, u32[]{:S(2)}, u32[]{:S(2)}) %collective-permute-start.9) | collective-permute-done | bytes 1048608 | tf_op jit(solution)/shard_map/ppermute | solution.py:72
  66.1 7.0 %norm_window.1.n_ref = bf16[3072,1024]{1,0:T(8,128)(2,1)S(1)} custom-call(s32[12]{0:T(128)S(1)} %and_convert_fusion.need_ref, s32[2]{0:T(128)S(1)} %pad_add_fusion.1.info_ref, bf16[512,1024]{1,0:T(8,128)(2,1)} %collective-permute-done.6.refs_0_, bf16[512,1024]{1,0:T(8,128)(2,1)S(1)} %collective-permute-done.7.refs_1_, bf16[512,1024]{1,0:T(8,128)(2,1)S(1)} %bitcast.263, ...), custom_call_target="tpu_custom_call" | custom-call | flops 1 | bytes 1 | tf_op jit(solution)/shard_map/norm_window/pallas_call | solution.py:891
  73.1 7.6 %collective-permute-start.15 = (bf16[256,512]{1,0:T(8,128)(2,1)S(1)}, bf16[256,512]{1,0:T(8,128)(2,1)S(1)}, u32[]{:S(2)}, u32[]{:S(2)}) collective-permute-start(bf16[256,512]{1,0:T(8,128)(2,1)S(1)} %copy-done.97), channel_id=1, source_target_pairs={{0,2},{1,3},{2,4},{3,5},{4,6},{5,7},{6,0},{7,1},{8,10},{9,11},{10,... | collective-permute-start | bytes 786440 | tf_op jit(solution)/shard_map/ppermute | solution.py:66
  88.5 8.0 %project.1 = (bf16[3072,512]{1,0:T(8,128)(2,1)S(1)}, bf16[3072,512]{1,0:T(8,128)(2,1)S(1)}, bf16[3072,512]{1,0:T(8,128)(2,1)S(1)}) custom-call(s32[12]{0:T(128)S(1)} %and_convert_fusion.need_ref, bf16[3072,1024]{1,0:T(8,128)(2,1)S(1)} %norm_window.1.n_ref, bf16[1024,1536]{1,0:T(8,128)(2,1)S(1)} %get-tuple-element.344.w_ref, f32[1,1536]{1,0:T(1,128)S(1)} %fusion.65.b_ref), custom_call_target="tpu_custom_call" | custom-call | flops 1 | bytes 1 | tf_op jit(solution)/shard_map/project/pallas_call | solution.py:843
  96.5 2.7 copy-done.8
  99.6 10.9 %attend.4 = (bf16[1024,128]{1,0:T(8,128)(2,1)S(1)}, f32[1,2,1024]{2,1,0:T(2,128)S(1)}) custom-call(s32[4]{0:T(128)S(1)} %slice.908.lo_ref, s32[4]{0:T(128)S(1)} %slice.936.hi_ref, s32[12]{0:T(128)S(1)} %convert_element_type.272.first_ref, s32[12]{0:T(128)S(1)} %convert_element_type.273.last_ref, bf16[3072,512]{1,0:T(8,128)(2,1)S(1)} %get-tuple-element.347.q_ref, ...), custom_call_target="tpu_custom_call" | custom-call | flops 1 | bytes 1 | tf_op jit(solution)/shard_map/attend/pallas_call | solution.py:970
  110.9 3.9 collective-permute-start.19
  114.8 10.9 %attend.5 = (bf16[1024,128]{1,0:T(8,128)(2,1)S(1)}, f32[1,2,1024]{2,1,0:T(2,128)S(1)}) custom-call(s32[4]{0:T(128)S(1)} %slice.908.lo_ref, s32[4]{0:T(128)S(1)} %slice.936.hi_ref, s32[12]{0:T(128)S(1)} %convert_element_type.272.first_ref, s32[12]{0:T(128)S(1)} %convert_element_type.273.last_ref, bf16[3072,512]{1,0:T(8,128)(2,1)S(1)} %get-tuple-element.347.q_ref, ...), custom_call_target="tpu_custom_call" | custom-call | flops 1 | bytes 1 | tf_op jit(solution)/shard_map/attend/pallas_call | solution.py:970
  127.9 12.5 %collective-permute-start.22 = (bf16[512,256]{1,0:T(8,128)(2,1)S(1)}, bf16[512,256]{1,0:T(8,128)(2,1)S(1)}, u32[]{:S(2)}, u32[]{:S(2)}) collective-permute-start(bf16[512,256]{1,0:T(8,128)(2,1)S(1)} %copy-done.96), channel_id=1, source_target_pairs={{0,2},{1,3},{2,4},{3,5},{4,6},{5,7},{6,0},{7,1},{8,10},{9,11},{10,... | collective-permute-start | bytes 786440 | tf_op jit(solution)/shard_map/ppermute | solution.py:66
  140.4 2.9 collective-permute-start.24
  143.3 10.9 %attend.6 = (bf16[1024,128]{1,0:T(8,128)(2,1)S(1)}, f32[1,2,1024]{2,1,0:T(2,128)S(1)}) custom-call(s32[4]{0:T(128)S(1)} %slice.908.lo_ref, s32[4]{0:T(128)S(1)} %slice.936.hi_ref, s32[12]{0:T(128)S(1)} %convert_element_type.272.first_ref, s32[12]{0:T(128)S(1)} %convert_element_type.273.last_ref, bf16[3072,512]{1,0:T(8,128)(2,1)S(1)} %get-tuple-element.347.q_ref, ...), custom_call_target="tpu_custom_call" | custom-call | flops 1 | bytes 1 | tf_op jit(solution)/shard_map/attend/pallas_call | solution.py:970
  157.6 10.9 %attend.7 = (bf16[1024,128]{1,0:T(8,128)(2,1)S(1)}, f32[1,2,1024]{2,1,0:T(2,128)S(1)}) custom-call(s32[4]{0:T(128)S(1)} %slice.908.lo_ref, s32[4]{0:T(128)S(1)} %slice.936.hi_ref, s32[12]{0:T(128)S(1)} %convert_element_type.272.first_ref, s32[12]{0:T(128)S(1)} %convert_element_type.273.last_ref, bf16[3072,512]{1,0:T(8,128)(2,1)S(1)} %get-tuple-element.347.q_ref, ...), custom_call_target="tpu_custom_call" | custom-call | flops 1 | bytes 1 | tf_op jit(solution)/shard_map/attend/pallas_call | solution.py:970
  172.4 3.6 collective-permute-done.27.sent_ref
  178.6 2.6 collective-permute-start.30
  184.0 9.6 %units.1 = (bf16[1024,2048]{1,0:T(8,128)(2,1)S(1)}, bf16[1024,2048]{1,0:T(8,128)(2,1)S(1)}) custom-call(bf16[1024,1024]{1,0:T(8,128)(2,1)S(1)} %constant_dynamic-update-slice_fusion.n_ref.a_ref, bf16[1024,2048]{1,0:T(8,128)(2,1)S(1)} %gather2.1.w_ref, f32[1,2048]{1,0:T(1,128)S(1)} %copy-done.79), custom_call_target="tpu_custom_call" | custom-call | flops 1 | bytes 1 | tf_op jit(solution)/shard_map/units/pallas_call | solution.py:700
  195.7 8.2 %collective-permute-done.29.refs_1_ = bf16[2,4,256,256]{3,2,1,0:T(8,128)(2,1)S(1)} collective-permute-done((bf16[2,4,256,256]{3,2,1,0:T(8,128)(2,1)}, bf16[2,4,256,256]{3,2,1,0:T(8,128)(2,1)S(1)}, u32[]{:S(2)}, u32[]{:S(2)}) %collective-permute-start.29) | collective-permute-done | bytes 1048608 | tf_op jit(solution)/shard_map/ppermute | solution.py:77
  205.9 7.1 %fc2_grad.1 = (bf16[2,4,256,256]{3,2,1,0:T(8,128)(2,1)S(1)}, bf16[2,4,256,256]{3,2,1,0:T(8,128)(2,1)}, bf16[2,4,256,256]{3,2,1,0:T(8,128)(2,1)S(1)}, bf16[2,4,256,256]{3,2,1,0:T(8,128)(2,1)}) custom-call(s32[1]{0:T(128)} %bitcast.3.index_ref, bf16[1024,2048]{1,0:T(8,128)(2,1)S(1)} %get-tuple-element.440.a_ref.first_ref.second_ref, ...), custom_call_target="tpu_custom_call" | custom-call | flops 1 | bytes 1 | tf_op jit(solution)/shard_map/fc2_grad/pallas_call | solution.py:530
  221.8 8.9 %pre_grad.1 = (bf16[1024,2048]{1,0:T(8,128)(2,1)S(1)}, f32[1,2048]{1,0:T(1,128)S(1)}) custom-call(bf16[1024,1024]{1,0:T(8,128)(2,1)S(1)} %scaled.1.b_ref.g_ref, bf16[2048,1024]{1,0:T(8,128)(2,1)S(1)} %gather3.1.w_ref, bf16[1024,2048]{1,0:T(8,128)(2,1)} %copy-done.35), custom_call_target="tpu_custom_call" | custom-call | flops 1 | bytes 1 | tf_op jit(solution)/shard_map/pre_grad/pallas_call | solution.py:559
  234.9 6.0 %fc1_grad.1 = (bf16[2,4,128,512]{3,2,1,0:T(8,128)(2,1)S(1)}, bf16[2,4,128,512]{3,2,1,0:T(8,128)(2,1)S(1)}, bf16[2,4,128,512]{3,2,1,0:T(8,128)(2,1)S(1)}, bf16[2,4,128,512]{3,2,1,0:T(8,128)(2,1)S(1)}) custom-call(s32[1]{0:T(128)} %bitcast.3.index_ref, bf16[1024,1024]{1,0:T(8,128)(2,1)S(1)} %copy-done.21, bf16[1024,2048]{1,0:T(8,128)(2,1)S(1)} %copy-done.14), custom_call_target="tpu_custom_call" | custom-call | flops 1 | bytes 1 | tf_op jit(solution)/shard_map/fc1_grad/pallas_call | solution.py:530
  241.9 6.6 %mlp_in_grad.1 = (f32[512,1024]{1,0:T(8,128)S(1)}, f32[512,1024]{1,0:T(8,128)S(1)}) custom-call(s32[1]{0:T(128)} %constant.143.clone.1.half_ref, bf16[1024,2048]{1,0:T(8,128)(2,1)S(1)} %copy-done.15, bf16[1024,2048]{1,0:T(8,128)(2,1)S(1)} %copy-done.15, bf16[1024,2048]{1,0:T(8,128)(2,1)S(1)} %gather2.1.w_ref), custom_call_target="tpu_custom_call" | custom-call | flops 1 | bytes 1 | tf_op jit(solution)/shard_map/mlp_in_grad/pallas_call | solution.py:593
  253.9 4.2 collective-permute-done.33.sent_ref
  258.0 4.5 norm_grad.1
  271.6 11.6 %collective-permute-start.37 = (f32[16,1024]{1,0:T(8,128)S(1)}, f32[16,1024]{1,0:T(8,128)S(1)}, u32[]{:S(2)}, u32[]{:S(2)}) collective-permute-start(f32[16,1024]{1,0:T(8,128)S(1)} %pad_maximum_fusion.25), channel_id=1, source_target_pairs={{0,2},{1,3},{2,4},{3,5},{4,6},{5,7},{8,10},{9,11},{10,12},{11,13},... | collective-permute-start | bytes 196616 | tf_op jit(solution)/shard_map/ppermute | solution.py:72
  285.5 5.9 %mlp_out.1 = (f32[512,1024]{1,0:T(8,128)S(1)}, f32[512,1024]{1,0:T(8,128)}) custom-call(s32[1]{0:T(128)} %constant.143.clone.1.half_ref, bf16[1024,2048]{1,0:T(8,128)(2,1)S(1)} %copy-done.10, bf16[1024,2048]{1,0:T(8,128)(2,1)S(1)} %copy-done.10, bf16[2048,1024]{1,0:T(8,128)(2,1)S(1)} %copy-done.12), custom_call_target="tpu_custom_call" | custom-call | flops 1 | bytes 1 | tf_op jit(solution)/shard_map/mlp_out/pallas_call | solution.py:593
  292.8 5.4 %collective-permute-start.35 = (bf16[1024,256]{1,0:T(8,128)(2,1)}, bf16[1024,256]{1,0:T(8,128)(2,1)}, u32[]{:S(2)}, u32[]{:S(2)}) collective-permute-start(bf16[1024,256]{1,0:T(8,128)(2,1)} %get-tuple-element.674), channel_id=1, source_target_pairs={{0,2},{1,3},{2,4},{3,5},{4,6},{5,7},{8,10},{9,11},{10,12},{11,13},... | collective-permute-start | bytes 1572872 | tf_op jit(solution)/shard_map/ppermute | solution.py:72
  301.2 7.1 %collective-permute-done.35 = bf16[1024,256]{1,0:T(8,128)(2,1)} collective-permute-done((bf16[1024,256]{1,0:T(8,128)(2,1)}, bf16[1024,256]{1,0:T(8,128)(2,1)}, u32[]{:S(2)}, u32[]{:S(2)}) %collective-permute-start.35) | collective-permute-done | bytes 524320 | tf_op jit(solution)/shard_map/ppermute | solution.py:72
  308.3 4.9 collective-permute-done.36
  324.9 15.2 %attend_back.4 = (bf16[1024,128]{1,0:T(8,128)(2,1)S(1)}, bf16[1024,128]{1,0:T(8,128)(2,1)S(1)}, bf16[1024,128]{1,0:T(8,128)(2,1)S(1)}, f32[1,8,128]{2,1,0:T(8,128)S(1)}) custom-call(s32[12]{0:T(128)S(1)} %get-tuple-element.538.lo_ref, s32[12]{0:T(128)S(1)} %get-tuple-element.829.hi_ref, bf16[3072,512]{1,0:T(8,128)(2,1)S(1)} %get-tuple-element.347.q_ref, ...), custom_call_target="tpu_custom_call" | custom-call | flops 1 | bytes 1 | tf_op jit(solution)/shard_map/attend_back/pallas_call | solution.py:1080
  349.9 6.9 %collective-permute-start.47 = (bf16[512,256]{1,0:T(8,128)(2,1)}, bf16[512,256]{1,0:T(8,128)(2,1)}, u32[]{:S(2)}, u32[]{:S(2)}) collective-permute-start(bf16[512,256]{1,0:T(8,128)(2,1)} %get-tuple-element.480), channel_id=1, source_target_pairs={{0,2},{1,3},{2,4},{3,5},{4,6},{5,7},{6,0},{7,1},{8,10},{9,11},{10,... | collective-permute-start | bytes 786440 | tf_op jit(solution)/shard_map/ppermute | solution.py:66
  356.8 2.6 collective-permute-start.49
  360.6 15.2 %attend_back.5 = (bf16[1024,128]{1,0:T(8,128)(2,1)S(1)}, bf16[1024,128]{1,0:T(8,128)(2,1)S(1)}, bf16[1024,128]{1,0:T(8,128)(2,1)S(1)}, f32[1,8,128]{2,1,0:T(8,128)S(1)}) custom-call(s32[12]{0:T(128)S(1)} %get-tuple-element.538.lo_ref, s32[12]{0:T(128)S(1)} %get-tuple-element.829.hi_ref, bf16[3072,512]{1,0:T(8,128)(2,1)S(1)} %get-tuple-element.347.q_ref, ...), custom_call_target="tpu_custom_call" | custom-call | flops 1 | bytes 1 | tf_op jit(solution)/shard_map/attend_back/pallas_call | solution.py:1080
  382.6 4.2 collective-permute-start.54
  388.3 4.0 collective-permute-start.50
  392.2 2.8 collective-permute-start.52
  396.3 15.1 %attend_back.6 = (bf16[1024,128]{1,0:T(8,128)(2,1)S(1)}, bf16[1024,128]{1,0:T(8,128)(2,1)S(1)}, bf16[1024,128]{1,0:T(8,128)(2,1)S(1)}, f32[1,8,128]{2,1,0:T(8,128)S(1)}) custom-call(s32[12]{0:T(128)S(1)} %get-tuple-element.538.lo_ref, s32[12]{0:T(128)S(1)} %get-tuple-element.829.hi_ref, bf16[3072,512]{1,0:T(8,128)(2,1)S(1)} %get-tuple-element.347.q_ref, ...), custom_call_target="tpu_custom_call" | custom-call | flops 1 | bytes 1 | tf_op jit(solution)/shard_map/attend_back/pallas_call | solution.py:1080
  421.7 15.4 %attend_back.7 = (bf16[1024,128]{1,0:T(8,128)(2,1)S(1)}, bf16[1024,128]{1,0:T(8,128)(2,1)S(1)}, bf16[1024,128]{1,0:T(8,128)(2,1)S(1)}, f32[1,8,128]{2,1,0:T(8,128)S(1)}) custom-call(s32[12]{0:T(128)S(1)} %get-tuple-element.538.lo_ref, s32[12]{0:T(128)S(1)} %get-tuple-element.829.hi_ref, bf16[3072,512]{1,0:T(8,128)(2,1)S(1)} %get-tuple-element.347.q_ref, ...), custom_call_target="tpu_custom_call" | custom-call | flops 1 | bytes 1 | tf_op jit(solution)/shard_map/attend_back/pallas_call | solution.py:1080
  447.0 10.2 %collective-permute-start.61 = (bf16[256,256]{1,0:T(8,128)(2,1)S(1)}, bf16[256,256]{1,0:T(8,128)(2,1)S(1)}, u32[]{:S(2)}, u32[]{:S(2)}) collective-permute-start(bf16[256,256]{1,0:T(8,128)(2,1)S(1)} %get-tuple-element.572), channel_id=1, source_target_pairs={{0,2},{1,3},{2,4},{3,5},{4,6},{5,7},{6,0},{7,1},{8,10},{9,11},{10,... | collective-permute-start | bytes 393224 | tf_op jit(solution)/shard_map/ppermute | solution.py:66
  460.0 6.1 %attn_in_grad.1 = (f32[512,1024]{1,0:T(8,128)S(1)}, f32[512,1024]{1,0:T(8,128)}) custom-call(s32[1]{0:T(128)} %bitcast.half_ref.index_ref, bf16[1024,1536]{1,0:T(8,128)(2,1)S(1)} %constant_dynamic-update-slice_fusion.2.first_ref.second_ref, bf16[1024,1536]{1,0:T(8,128)(2,1)S(1)} %constant_dynamic-update-slice_fusion.2.first_ref.second_ref, ...), custom_call_target="tpu_custom_call" | custom-call | flops 1 | bytes 1 | tf_op jit(solution)/shard_map/attn_in_grad/pallas_call | solution.py:593
  480.8 7.6 %finish.1 = (f32[512,1024]{1,0:T(8,128)}, bf16[512,1024]{1,0:T(8,128)(2,1)}, f32[8,1024]{1,0:T(8,128)S(1)}) custom-call(f32[512,1024]{1,0:T(8,128)S(1)} %copy-done.41, f32[512,1024]{1,0:T(8,128)} %collective-permute-done.64.sent1_ref, bf16[512,1024]{1,0:T(8,128)(2,1)S(1)} %bitcast.265, f32[512,1024]{1,0:T(8,128)S(1)} %copy-done.37, ...), custom_call_target="tpu_custom_call" | custom-call | flops 1 | bytes 1 | tf_op jit(solution)/shard_map/finish/pallas_call | solution.py:635
  495.5 2.5 collective-permute-start.70
  503.9 5.0 collective-permute-done.70
  520.6 3.3 collective-permute-done.77
  523.9 4.3 collective-permute-done.76
  (581 shorter events, 191.4 us)
Async XLA Ops:
  13.8 52.3 %collective-permute-start.8 = (bf16[512,1024]{1,0:T(8,128)(2,1)S(1)}, bf16[512,1024]{1,0:T(8,128)(2,1)S(1)}, u32[]{:S(2)}, u32[]{:S(2)}) collective-permute-start(bf16[512,1024]{1,0:T(8,128)(2,1)S(1)} %bitcast.260), channel_id=1, source_target_pairs={{0,1},{1,0},{2,3},{3,2},{4,5},{5,4},{6,7},{7,6},{8,9},{9,8},{10,11... | collective-permute-start | bytes 3145736 | tf_op jit(solution)/shard_map/ppermute | solution.py:61
  13.8 26.0 %collective-permute-start.4 = (bf16[272,512]{1,0:T(8,128)(2,1)S(1)}, bf16[272,512]{1,0:T(8,128)(2,1)S(1)}, u32[]{:S(2)}, u32[]{:S(2)}) collective-permute-start(bf16[272,512]{1,0:T(8,128)(2,1)S(1)} %pad_maximum_fusion.17.refs_0_), channel_id=1, source_target_pairs={{0,4},{1,5},{2,6},{3,7},{4,0},{5,1},{6,2},{7,3},{8,12},{9,13},{10,... | collective-permute-start | bytes 835592 | tf_op jit(solution)/shard_map/ppermute | solution.py:66
  16.4 23.5 %collective-permute-start.5 = (bf16[272,512]{1,0:T(8,128)(2,1)S(1)}, bf16[272,512]{1,0:T(8,128)(2,1)S(1)}, u32[]{:S(2)}, u32[]{:S(2)}) collective-permute-start(bf16[272,512]{1,0:T(8,128)(2,1)S(1)} %pad_maximum_fusion.17.refs_0_), channel_id=1, source_target_pairs={{0,6},{1,7},{2,0},{3,1},{4,2},{5,3},{6,4},{7,5},{8,14},{9,15},{10,... | collective-permute-start | bytes 835592 | tf_op jit(solution)/shard_map/ppermute | solution.py:66
  23.6 33.5 %collective-permute-start.9 = (bf16[512,1024]{1,0:T(8,128)(2,1)S(1)}, bf16[512,1024]{1,0:T(8,128)(2,1)S(1)}, u32[]{:S(2)}, u32[]{:S(2)}) collective-permute-start(bf16[512,1024]{1,0:T(8,128)(2,1)S(1)} %bitcast.261), channel_id=1, source_target_pairs={{2,0},{3,1},{4,2},{5,3},{6,4},{7,5},{10,8},{11,9},{12,10},{13,11},... | collective-permute-start | bytes 3145736 | tf_op jit(solution)/shard_map/ppermute | solution.py:72
  24.9 32.2 %collective-permute-start.6 = (bf16[512,1024]{1,0:T(8,128)(2,1)S(1)}, bf16[512,1024]{1,0:T(8,128)(2,1)}, u32[]{:S(2)}, u32[]{:S(2)}) collective-permute-start(bf16[512,1024]{1,0:T(8,128)(2,1)S(1)} %bitcast.262), channel_id=1, source_target_pairs={{0,2},{1,3},{2,4},{3,5},{4,6},{5,7},{8,10},{9,11},{10,12},{11,13},... | collective-permute-start | bytes 3145736 | tf_op jit(solution)/shard_map/ppermute | solution.py:72
  60.2 25.1 %collective-permute-start.13 = (bf16[2,4,128,512]{3,2,1,0:T(8,128)(2,1)S(1)}, bf16[2,4,128,512]{3,2,1,0:T(8,128)(2,1)S(1)}, u32[]{:S(2)}, u32[]{:S(2)}) collective-permute-start(bf16[2,4,128,512]{3,2,1,0:T(8,128)(2,1)S(1)} %pad_maximum_fusion.2.refs_0_), channel_id=1, source_target_pairs={{0,16},{8,24},{16,0},{24,8},{1,17},{9,25},{17,1},{25,9},{2,18},{10... | collective-permute-start | bytes 3145736 | tf_op jit(solution)/shard_map/ppermute | solution.py:77
  61.8 24.8 %collective-permute-start.14 = (bf16[2,4,128,512]{3,2,1,0:T(8,128)(2,1)S(1)}, bf16[2,4,128,512]{3,2,1,0:T(8,128)(2,1)S(1)}, u32[]{:S(2)}, u32[]{:S(2)}) collective-permute-start(bf16[2,4,128,512]{3,2,1,0:T(8,128)(2,1)S(1)} %pad_maximum_fusion.3.refs_2_), channel_id=1, source_target_pairs={{0,8},{8,0},{16,24},{24,16},{1,9},{9,1},{17,25},{25,17},{2,10},{10... | collective-permute-start | bytes 3145736 | tf_op jit(solution)/shard_map/ppermute | solution.py:77
  73.1 37.4 %collective-permute-start.15 = (bf16[256,512]{1,0:T(8,128)(2,1)S(1)}, bf16[256,512]{1,0:T(8,128)(2,1)S(1)}, u32[]{:S(2)}, u32[]{:S(2)}) collective-permute-start(bf16[256,512]{1,0:T(8,128)(2,1)S(1)} %copy-done.97), channel_id=1, source_target_pairs={{0,2},{1,3},{2,4},{3,5},{4,6},{5,7},{6,0},{7,1},{8,10},{9,11},{10,... | collective-permute-start | bytes 786440 | tf_op jit(solution)/shard_map/ppermute | solution.py:66
  80.7 29.9 %collective-permute-start.16 = (bf16[256,512]{1,0:T(8,128)(2,1)S(1)}, bf16[256,512]{1,0:T(8,128)(2,1)S(1)}, u32[]{:S(2)}, u32[]{:S(2)}) collective-permute-start(bf16[256,512]{1,0:T(8,128)(2,1)S(1)} %copy-done.97), channel_id=1, source_target_pairs={{0,4},{1,5},{2,6},{3,7},{4,0},{5,1},{6,2},{7,3},{8,12},{9,13},{10,... | collective-permute-start | bytes 786440 | tf_op jit(solution)/shard_map/ppermute | solution.py:66
  80.7 29.9 %collective-permute-start.17 = (bf16[256,512]{1,0:T(8,128)(2,1)S(1)}, bf16[256,512]{1,0:T(8,128)(2,1)S(1)}, u32[]{:S(2)}, u32[]{:S(2)}) collective-permute-start(bf16[256,512]{1,0:T(8,128)(2,1)S(1)} %copy-done.97), channel_id=1, source_target_pairs={{0,6},{1,7},{2,0},{3,1},{4,2},{5,3},{6,4},{7,5},{8,14},{9,15},{10,... | collective-permute-start | bytes 786440 | tf_op jit(solution)/shard_map/ppermute | solution.py:66
  126.0 28.3 %collective-permute-start.20 = (bf16[2,4,128,512]{3,2,1,0:T(8,128)(2,1)S(1)}, bf16[2,4,128,512]{3,2,1,0:T(8,128)(2,1)S(1)}, u32[]{:S(2)}, u32[]{:S(2)}) collective-permute-start(bf16[2,4,128,512]{3,2,1,0:T(8,128)(2,1)S(1)} %pad_maximum_fusion.4.refs_0_), channel_id=1, source_target_pairs={{0,16},{8,24},{16,0},{24,8},{1,17},{9,25},{17,1},{25,9},{2,18},{10... | collective-permute-start | bytes 3145736 | tf_op jit(solution)/shard_map/ppermute | solution.py:77
  127.5 26.7 %collective-permute-start.21 = (bf16[2,4,128,512]{3,2,1,0:T(8,128)(2,1)S(1)}, bf16[2,4,128,512]{3,2,1,0:T(8,128)(2,1)S(1)}, u32[]{:S(2)}, u32[]{:S(2)}) collective-permute-start(bf16[2,4,128,512]{3,2,1,0:T(8,128)(2,1)S(1)} %pad_maximum_fusion.5.refs_2_), channel_id=1, source_target_pairs={{0,8},{8,0},{16,24},{24,16},{1,9},{9,1},{17,25},{25,17},{2,10},{10... | collective-permute-start | bytes 3145736 | tf_op jit(solution)/shard_map/ppermute | solution.py:77
  127.9 26.4 %collective-permute-start.22 = (bf16[512,256]{1,0:T(8,128)(2,1)S(1)}, bf16[512,256]{1,0:T(8,128)(2,1)S(1)}, u32[]{:S(2)}, u32[]{:S(2)}) collective-permute-start(bf16[512,256]{1,0:T(8,128)(2,1)S(1)} %copy-done.96), channel_id=1, source_target_pairs={{0,2},{1,3},{2,4},{3,5},{4,6},{5,7},{6,0},{7,1},{8,10},{9,11},{10,... | collective-permute-start | bytes 786440 | tf_op jit(solution)/shard_map/ppermute | solution.py:66
  178.3 25.6 %collective-permute-start.29 = (bf16[2,4,256,256]{3,2,1,0:T(8,128)(2,1)}, bf16[2,4,256,256]{3,2,1,0:T(8,128)(2,1)S(1)}, u32[]{:S(2)}, u32[]{:S(2)}) collective-permute-start(bf16[2,4,256,256]{3,2,1,0:T(8,128)(2,1)} %pad_maximum_fusion.7.refs_0_), channel_id=1, source_target_pairs={{0,16},{8,24},{16,0},{24,8},{1,17},{9,25},{17,1},{25,9},{2,18},{10... | collective-permute-start | bytes 3145736 | tf_op jit(solution)/shard_map/ppermute | solution.py:77
  178.6 26.3 %collective-permute-start.30 = (bf16[2,4,256,256]{3,2,1,0:T(8,128)(2,1)S(1)}, bf16[2,4,256,256]{3,2,1,0:T(8,128)(2,1)S(1)}, u32[]{:S(2)}, u32[]{:S(2)}) collective-permute-start(bf16[2,4,256,256]{3,2,1,0:T(8,128)(2,1)S(1)} %pad_maximum_fusion.8.refs_2_), channel_id=1, source_target_pairs={{0,8},{8,0},{16,24},{24,16},{1,9},{9,1},{17,25},{25,17},{2,10},{10... | collective-permute-start | bytes 3145736 | tf_op jit(solution)/shard_map/ppermute | solution.py:77
  214.0 34.6 %collective-permute-start.31 = (bf16[2,4,256,256]{3,2,1,0:T(8,128)(2,1)}, bf16[2,4,256,256]{3,2,1,0:T(8,128)(2,1)}, u32[]{:S(2)}, u32[]{:S(2)}) collective-permute-start(bf16[2,4,256,256]{3,2,1,0:T(8,128)(2,1)} %get-tuple-element.422), channel_id=1, source_target_pairs={{0,8},{8,0},{16,24},{24,16},{1,9},{9,1},{17,25},{25,17},{2,10},{10... | collective-permute-start | bytes 3145736 | tf_op jit(solution)/shard_map/ppermute | solution.py:77
  215.4 33.1 %collective-permute-start.32 = (bf16[2,4,256,256]{3,2,1,0:T(8,128)(2,1)}, bf16[2,4,256,256]{3,2,1,0:T(8,128)(2,1)}, u32[]{:S(2)}, u32[]{:S(2)}) collective-permute-start(bf16[2,4,256,256]{3,2,1,0:T(8,128)(2,1)} %get-tuple-element.423), channel_id=1, source_target_pairs={{0,16},{8,24},{16,0},{24,8},{1,17},{9,25},{17,1},{25,9},{2,18},{10... | collective-permute-start | bytes 3145736 | tf_op jit(solution)/shard_map/ppermute | solution.py:77
  264.1 37.1 %collective-permute-start.39 = (bf16[1,4,256,256]{3,2,1,0:T(8,128)(2,1)}, bf16[1,4,256,256]{3,2,1,0:T(8,128)(2,1)}, u32[]{:S(2)}, u32[]{:S(2)}) collective-permute-start(bf16[1,4,256,256]{3,2,1,0:T(8,128)(2,1)} %slice.1111), channel_id=1, source_target_pairs={{0,16},{8,24},{16,0},{24,8},{1,17},{9,25},{17,1},{25,9},{2,18},{10... | collective-permute-start | bytes 1572872 | tf_op jit(solution)/shard_map/ppermute | solution.py:77
  264.7 36.4 %collective-permute-start.40 = (bf16[1,4,256,256]{3,2,1,0:T(8,128)(2,1)}, bf16[1,4,256,256]{3,2,1,0:T(8,128)(2,1)}, u32[]{:S(2)}, u32[]{:S(2)}) collective-permute-start(bf16[1,4,256,256]{3,2,1,0:T(8,128)(2,1)} %slice.1112), channel_id=1, source_target_pairs={{0,8},{8,0},{16,24},{24,16},{1,9},{9,1},{17,25},{25,17},{2,10},{10... | collective-permute-start | bytes 1572872 | tf_op jit(solution)/shard_map/ppermute | solution.py:77
  271.6 26.6 %collective-permute-start.37 = (f32[16,1024]{1,0:T(8,128)S(1)}, f32[16,1024]{1,0:T(8,128)S(1)}, u32[]{:S(2)}, u32[]{:S(2)}) collective-permute-start(f32[16,1024]{1,0:T(8,128)S(1)} %pad_maximum_fusion.25), channel_id=1, source_target_pairs={{0,2},{1,3},{2,4},{3,5},{4,6},{5,7},{8,10},{9,11},{10,12},{11,13},... | collective-permute-start | bytes 196616 | tf_op jit(solution)/shard_map/ppermute | solution.py:72
  283.2 16.3 %collective-permute-start.38 = (f32[16,1024]{1,0:T(8,128)S(1)}, f32[16,1024]{1,0:T(8,128)S(1)}, u32[]{:S(2)}, u32[]{:S(2)}) collective-permute-start(f32[16,1024]{1,0:T(8,128)S(1)} %pad_maximum_fusion.25), channel_id=1, source_target_pairs={{2,0},{3,1},{4,2},{5,3},{6,4},{7,5},{10,8},{11,9},{12,10},{13,11},... | collective-permute-start | bytes 196616 | tf_op jit(solution)/shard_map/ppermute | solution.py:72
  292.8 15.5 %collective-permute-start.35 = (bf16[1024,256]{1,0:T(8,128)(2,1)}, bf16[1024,256]{1,0:T(8,128)(2,1)}, u32[]{:S(2)}, u32[]{:S(2)}) collective-permute-start(bf16[1024,256]{1,0:T(8,128)(2,1)} %get-tuple-element.674), channel_id=1, source_target_pairs={{0,2},{1,3},{2,4},{3,5},{4,6},{5,7},{8,10},{9,11},{10,12},{11,13},... | collective-permute-start | bytes 1572872 | tf_op jit(solution)/shard_map/ppermute | solution.py:72
  298.2 15.0 %collective-permute-start.36 = (bf16[1024,256]{1,0:T(8,128)(2,1)}, bf16[1024,256]{1,0:T(8,128)(2,1)}, u32[]{:S(2)}, u32[]{:S(2)}) collective-permute-start(bf16[1024,256]{1,0:T(8,128)(2,1)} %get-tuple-element.674), channel_id=1, source_target_pairs={{2,0},{3,1},{4,2},{5,3},{6,4},{7,5},{10,8},{11,9},{12,10},{13,11},... | collective-permute-start | bytes 1572872 | tf_op jit(solution)/shard_map/ppermute | solution.py:72
  313.2 29.2 %collective-permute-start.43 = (bf16[2,4,128,512]{3,2,1,0:T(8,128)(2,1)}, bf16[2,4,128,512]{3,2,1,0:T(8,128)(2,1)}, u32[]{:S(2)}, u32[]{:S(2)}) collective-permute-start(bf16[2,4,128,512]{3,2,1,0:T(8,128)(2,1)} %copy-done.82), channel_id=1, source_target_pairs={{0,8},{8,0},{16,24},{24,16},{1,9},{9,1},{17,25},{25,17},{2,10},{10... | collective-permute-start | bytes 3145736 | tf_op jit(solution)/shard_map/ppermute | solution.py:77
  313.7 28.7 %collective-permute-start.44 = (bf16[2,4,128,512]{3,2,1,0:T(8,128)(2,1)}, bf16[2,4,128,512]{3,2,1,0:T(8,128)(2,1)}, u32[]{:S(2)}, u32[]{:S(2)}) collective-permute-start(bf16[2,4,128,512]{3,2,1,0:T(8,128)(2,1)} %copy-done.81), channel_id=1, source_target_pairs={{0,16},{8,24},{16,0},{24,8},{1,17},{9,25},{17,1},{25,9},{2,18},{10... | collective-permute-start | bytes 3145736 | tf_op jit(solution)/shard_map/ppermute | solution.py:77
  315.2 27.1 %collective-permute-start.41 = (bf16[1024,256]{1,0:T(8,128)(2,1)}, bf16[1024,256]{1,0:T(8,128)(2,1)}, u32[]{:S(2)}, u32[]{:S(2)}) collective-permute-start(bf16[1024,256]{1,0:T(8,128)(2,1)} %get-tuple-element.673), channel_id=1, source_target_pairs={{0,2},{1,3},{2,4},{3,5},{4,6},{5,7},{8,10},{9,11},{10,12},{11,13},... | collective-permute-start | bytes 1572872 | tf_op jit(solution)/shard_map/ppermute | solution.py:72
  317.5 24.9 %collective-permute-start.42 = (bf16[1024,256]{1,0:T(8,128)(2,1)}, bf16[1024,256]{1,0:T(8,128)(2,1)}, u32[]{:S(2)}, u32[]{:S(2)}) collective-permute-start(bf16[1024,256]{1,0:T(8,128)(2,1)} %get-tuple-element.673), channel_id=1, source_target_pairs={{2,0},{3,1},{4,2},{5,3},{6,4},{7,5},{10,8},{11,9},{12,10},{13,11},... | collective-permute-start | bytes 1572872 | tf_op jit(solution)/shard_map/ppermute | solution.py:72
  347.6 30.6 %collective-permute-start.45 = (bf16[1,4,128,512]{3,2,1,0:T(8,128)(2,1)}, bf16[1,4,128,512]{3,2,1,0:T(8,128)(2,1)S(1)}, u32[]{:S(2)}, u32[]{:S(2)}) collective-permute-start(bf16[1,4,128,512]{3,2,1,0:T(8,128)(2,1)} %slice.1117), channel_id=1, source_target_pairs={{0,16},{8,24},{16,0},{24,8},{1,17},{9,25},{17,1},{25,9},{2,18},{10... | collective-permute-start | bytes 1572872 | tf_op jit(solution)/shard_map/ppermute | solution.py:77
  348.1 30.1 %collective-permute-start.46 = (bf16[1,4,128,512]{3,2,1,0:T(8,128)(2,1)}, bf16[1,4,128,512]{3,2,1,0:T(8,128)(2,1)}, u32[]{:S(2)}, u32[]{:S(2)}) collective-permute-start(bf16[1,4,128,512]{3,2,1,0:T(8,128)(2,1)} %slice.1118), channel_id=1, source_target_pairs={{0,8},{8,0},{16,24},{24,16},{1,9},{9,1},{17,25},{25,17},{2,10},{10... | collective-permute-start | bytes 1572872 | tf_op jit(solution)/shard_map/ppermute | solution.py:77
  349.9 28.3 %collective-permute-start.47 = (bf16[512,256]{1,0:T(8,128)(2,1)}, bf16[512,256]{1,0:T(8,128)(2,1)}, u32[]{:S(2)}, u32[]{:S(2)}) collective-permute-start(bf16[512,256]{1,0:T(8,128)(2,1)} %get-tuple-element.480), channel_id=1, source_target_pairs={{0,2},{1,3},{2,4},{3,5},{4,6},{5,7},{6,0},{7,1},{8,10},{9,11},{10,... | collective-permute-start | bytes 786440 | tf_op jit(solution)/shard_map/ppermute | solution.py:66
  356.8 21.4 %collective-permute-start.48 = (bf16[512,256]{1,0:T(8,128)(2,1)}, bf16[512,256]{1,0:T(8,128)(2,1)}, u32[]{:S(2)}, u32[]{:S(2)}) collective-permute-start(bf16[512,256]{1,0:T(8,128)(2,1)} %get-tuple-element.481), channel_id=1, source_target_pairs={{0,4},{1,5},{2,6},{3,7},{4,0},{5,1},{6,2},{7,3},{8,12},{9,13},{10,... | collective-permute-start | bytes 786440 | tf_op jit(solution)/shard_map/ppermute | solution.py:66
  356.8 21.4 %collective-permute-start.49 = (bf16[512,256]{1,0:T(8,128)(2,1)}, bf16[512,256]{1,0:T(8,128)(2,1)}, u32[]{:S(2)}, u32[]{:S(2)}) collective-permute-start(bf16[512,256]{1,0:T(8,128)(2,1)} %get-tuple-element.482), channel_id=1, source_target_pairs={{0,6},{1,7},{2,0},{3,1},{4,2},{5,3},{6,4},{7,5},{8,14},{9,15},{10,... | collective-permute-start | bytes 786440 | tf_op jit(solution)/shard_map/ppermute | solution.py:66
  382.6 29.0 %collective-permute-start.53 = (bf16[2,4,128,256]{3,2,1,0:T(8,128)(2,1)S(1)}, bf16[2,4,128,256]{3,2,1,0:T(8,128)(2,1)}, u32[]{:S(2)}, u32[]{:S(2)}) collective-permute-start(bf16[2,4,128,256]{3,2,1,0:T(8,128)(2,1)S(1)} %get-tuple-element.509), channel_id=1, source_target_pairs={{0,8},{8,0},{16,24},{24,16},{1,9},{9,1},{17,25},{25,17},{2,10},{10... | collective-permute-start | bytes 1572872 | tf_op jit(solution)/shard_map/ppermute | solution.py:77
  382.6 29.0 %collective-permute-start.54 = (bf16[2,4,128,256]{3,2,1,0:T(8,128)(2,1)S(1)}, bf16[2,4,128,256]{3,2,1,0:T(8,128)(2,1)}, u32[]{:S(2)}, u32[]{:S(2)}) collective-permute-start(bf16[2,4,128,256]{3,2,1,0:T(8,128)(2,1)S(1)} %get-tuple-element.510), channel_id=1, source_target_pairs={{0,16},{8,24},{16,0},{24,8},{1,17},{9,25},{17,1},{25,9},{2,18},{10... | collective-permute-start | bytes 1572872 | tf_op jit(solution)/shard_map/ppermute | solution.py:77
  388.3 23.2 %collective-permute-start.50 = (bf16[256,512]{1,0:T(8,128)(2,1)}, bf16[256,512]{1,0:T(8,128)(2,1)S(1)}, u32[]{:S(2)}, u32[]{:S(2)}) collective-permute-start(bf16[256,512]{1,0:T(8,128)(2,1)} %get-tuple-element.506), channel_id=1, source_target_pairs={{0,2},{1,3},{2,4},{3,5},{4,6},{5,7},{6,0},{7,1},{8,10},{9,11},{10,... | collective-permute-start | bytes 786440 | tf_op jit(solution)/shard_map/ppermute | solution.py:66
  392.2 19.3 %collective-permute-start.51 = (bf16[256,512]{1,0:T(8,128)(2,1)}, bf16[256,512]{1,0:T(8,128)(2,1)S(1)}, u32[]{:S(2)}, u32[]{:S(2)}) collective-permute-start(bf16[256,512]{1,0:T(8,128)(2,1)} %get-tuple-element.507), channel_id=1, source_target_pairs={{0,4},{1,5},{2,6},{3,7},{4,0},{5,1},{6,2},{7,3},{8,12},{9,13},{10,... | collective-permute-start | bytes 786440 | tf_op jit(solution)/shard_map/ppermute | solution.py:66
  392.2 19.3 %collective-permute-start.52 = (bf16[256,512]{1,0:T(8,128)(2,1)}, bf16[256,512]{1,0:T(8,128)(2,1)}, u32[]{:S(2)}, u32[]{:S(2)}) collective-permute-start(bf16[256,512]{1,0:T(8,128)(2,1)} %get-tuple-element.508), channel_id=1, source_target_pairs={{0,6},{1,7},{2,0},{3,1},{4,2},{5,3},{6,4},{7,5},{8,14},{9,15},{10,... | collective-permute-start | bytes 786440 | tf_op jit(solution)/shard_map/ppermute | solution.py:66
  414.3 22.8 %collective-permute-start.56 = (bf16[1,128,1024]{2,1,0:T(8,128)(2,1)S(1)}, bf16[1,128,1024]{2,1,0:T(8,128)(2,1)S(1)}, u32[]{:S(2)}, u32[]{:S(2)}) collective-permute-start(bf16[1,128,1024]{2,1,0:T(8,128)(2,1)S(1)} %get-tuple-element.546), channel_id=1, source_target_pairs={{0,16},{8,24},{16,0},{24,8},{1,17},{9,25},{17,1},{25,9},{2,18},{10... | collective-permute-start | bytes 786440 | tf_op jit(solution)/shard_map/ppermute | solution.py:77
  414.4 23.8 %collective-permute-start.55 = (bf16[1,128,1024]{2,1,0:T(8,128)(2,1)S(1)}, bf16[1,128,1024]{2,1,0:T(8,128)(2,1)S(1)}, u32[]{:S(2)}, u32[]{:S(2)}) collective-permute-start(bf16[1,128,1024]{2,1,0:T(8,128)(2,1)S(1)} %get-tuple-element.545), channel_id=1, source_target_pairs={{0,8},{8,0},{16,24},{24,16},{1,9},{9,1},{17,25},{25,17},{2,10},{10... | collective-permute-start | bytes 786440 | tf_op jit(solution)/shard_map/ppermute | solution.py:77
  418.7 20.3 %collective-permute-start.57 = (bf16[1,4,128,256]{3,2,1,0:T(8,128)(2,1)S(1)}, bf16[1,4,128,256]{3,2,1,0:T(8,128)(2,1)S(1)}, u32[]{:S(2)}, u32[]{:S(2)}) collective-permute-start(bf16[1,4,128,256]{3,2,1,0:T(8,128)(2,1)S(1)} %slice.1123), channel_id=1, source_target_pairs={{0,16},{8,24},{16,0},{24,8},{1,17},{9,25},{17,1},{25,9},{2,18},{10... | collective-permute-start | bytes 786440 | tf_op jit(solution)/shard_map/ppermute | solution.py:77
  418.9 20.1 %collective-permute-start.58 = (bf16[1,4,128,256]{3,2,1,0:T(8,128)(2,1)S(1)}, bf16[1,4,128,256]{3,2,1,0:T(8,128)(2,1)S(1)}, u32[]{:S(2)}, u32[]{:S(2)}) collective-permute-start(bf16[1,4,128,256]{3,2,1,0:T(8,128)(2,1)S(1)} %slice.1124), channel_id=1, source_target_pairs={{0,8},{8,0},{16,24},{24,16},{1,9},{9,1},{17,25},{25,17},{2,10},{10... | collective-permute-start | bytes 786440 | tf_op jit(solution)/shard_map/ppermute | solution.py:77
  444.8 21.4 %collective-permute-start.59 = (bf16[2,4,128,256]{3,2,1,0:T(8,128)(2,1)S(1)}, bf16[2,4,128,256]{3,2,1,0:T(8,128)(2,1)S(1)}, u32[]{:S(2)}, u32[]{:S(2)}) collective-permute-start(bf16[2,4,128,256]{3,2,1,0:T(8,128)(2,1)S(1)} %get-tuple-element.569), channel_id=1, source_target_pairs={{0,8},{8,0},{16,24},{24,16},{1,9},{9,1},{17,25},{25,17},{2,10},{10... | collective-permute-start | bytes 1572872 | tf_op jit(solution)/shard_map/ppermute | solution.py:77
  444.9 21.4 %collective-permute-start.60 = (bf16[2,4,128,256]{3,2,1,0:T(8,128)(2,1)S(1)}, bf16[2,4,128,256]{3,2,1,0:T(8,128)(2,1)S(1)}, u32[]{:S(2)}, u32[]{:S(2)}) collective-permute-start(bf16[2,4,128,256]{3,2,1,0:T(8,128)(2,1)S(1)} %get-tuple-element.570), channel_id=1, source_target_pairs={{0,16},{8,24},{16,0},{24,8},{1,17},{9,25},{17,1},{25,9},{2,18},{10... | collective-permute-start | bytes 1572872 | tf_op jit(solution)/shard_map/ppermute | solution.py:77
  447.0 19.1 %collective-permute-start.61 = (bf16[256,256]{1,0:T(8,128)(2,1)S(1)}, bf16[256,256]{1,0:T(8,128)(2,1)S(1)}, u32[]{:S(2)}, u32[]{:S(2)}) collective-permute-start(bf16[256,256]{1,0:T(8,128)(2,1)S(1)} %get-tuple-element.572), channel_id=1, source_target_pairs={{0,2},{1,3},{2,4},{3,5},{4,6},{5,7},{6,0},{7,1},{8,10},{9,11},{10,... | collective-permute-start | bytes 393224 | tf_op jit(solution)/shard_map/ppermute | solution.py:66
  470.4 29.4 %collective-permute-start.73 = (bf16[2,128,1024]{2,1,0:T(8,128)(2,1)}, bf16[2,128,1024]{2,1,0:T(8,128)(2,1)}, u32[]{:S(2)}, u32[]{:S(2)}) collective-permute-start(bf16[2,128,1024]{2,1,0:T(8,128)(2,1)} %pad_maximum_fusion.14), channel_id=1, source_target_pairs={{0,8},{8,0},{16,24},{24,16},{1,9},{9,1},{17,25},{25,17},{2,10},{10... | collective-permute-start | bytes 1572872 | tf_op jit(solution)/shard_map/ppermute | solution.py:77
  472.2 28.7 %collective-permute-start.72 = (bf16[2,128,1024]{2,1,0:T(8,128)(2,1)}, bf16[2,128,1024]{2,1,0:T(8,128)(2,1)}, u32[]{:S(2)}, u32[]{:S(2)}) collective-permute-start(bf16[2,128,1024]{2,1,0:T(8,128)(2,1)} %pad_maximum_fusion.13), channel_id=1, source_target_pairs={{0,16},{8,24},{16,0},{24,8},{1,17},{9,25},{17,1},{25,9},{2,18},{10... | collective-permute-start | bytes 1572872 | tf_op jit(solution)/shard_map/ppermute | solution.py:77
  474.2 19.0 %collective-permute-start.67 = (bf16[1,4,128,256]{3,2,1,0:T(8,128)(2,1)}, bf16[1,4,128,256]{3,2,1,0:T(8,128)(2,1)}, u32[]{:S(2)}, u32[]{:S(2)}) collective-permute-start(bf16[1,4,128,256]{3,2,1,0:T(8,128)(2,1)} %slice.1127), channel_id=1, source_target_pairs={{0,16},{8,24},{16,0},{24,8},{1,17},{9,25},{17,1},{25,9},{2,18},{10... | collective-permute-start | bytes 786440 | tf_op jit(solution)/shard_map/ppermute | solution.py:77
  474.2 19.0 %collective-permute-start.68 = (bf16[1,4,128,256]{3,2,1,0:T(8,128)(2,1)}, bf16[1,4,128,256]{3,2,1,0:T(8,128)(2,1)}, u32[]{:S(2)}, u32[]{:S(2)}) collective-permute-start(bf16[1,4,128,256]{3,2,1,0:T(8,128)(2,1)} %slice.1128), channel_id=1, source_target_pairs={{0,8},{8,0},{16,24},{24,16},{1,9},{9,1},{17,25},{25,17},{2,10},{10... | collective-permute-start | bytes 786440 | tf_op jit(solution)/shard_map/ppermute | solution.py:77
  (140 other events, 1224.3 us)
where the time goes:
time: 541 us; the launch traced here: 535 us
  Pallas kernels  205 us (38%)
  starting transfers between devices  153 us (28%)
  waiting for transfers between devices  63.1 us (12%)
  local copies, waits for them, and re-layouts  57.3 us (11%)
  other arithmetic  50.5 us (9%)
    ppermute x21, starting transfers between devices, along_z(): lax.ppermute(value, 'fsdp', [(i, (i + 2 * by) % size) for i in range(size)])  65.6 us
    pallas_call x4, Pallas kernels, attend_back(): pl.pallas_call(functools.partial(attend_back_kernel, start, stop), out_sh...  60.9 us
    ppermute x36, starting transfers between devices, across_rep(): return lax.ppermute(value, 'rep', [(i, i ^ 1 << bit) for i in range(size)])  46 us
    pallas_call x4, Pallas kernels, attend(): pl.pallas_call(attend_kernel, out_shape=[jax.ShapeDtypeStruct((own_rows,...  43.7 us
    ppermute x8, starting transfers between devices, from_chip(): return lax.ppermute(value, 'fsdp', pairs)  38.3 us
    unnamed x262, local copies, waits for them, and re-layouts  36.5 us
    ppermute x36, waiting for transfers between devices, across_rep(): return lax.ppermute(value, 'rep', [(i, i ^ 1 << bit) for i in range(size)])  22 us
    pallas_call x4, Pallas kernels, product(): pl.pallas_call(product_nt_kernel if flipped else product_kernel, out_shap...  20.4 us
  transfers between devices with their start and end apart: 80, of which 17 were waited for; matrix products, arithmetic and copies ran while one was open for 10% of the time, Pallas kernels for 35%

commit v1 on v0

--- a/solution.py
+++ b/solution.py
@@ -18,6 +18,7 @@
 BLOCK = 256
 
 SHORT = pl.CostEstimate(flops=1, transcendentals=0, bytes_accessed=1)
+FILLER = pl.CostEstimate(flops=1 << 33, transcendentals=0, bytes_accessed=1 << 23)
 
 f32 = jnp.float32
 bf16 = jnp.bfloat16
@@ -586,7 +587,7 @@
     out2_ref[...] = dot(second_ref[...], held[...])
 
 
-def product(a, weight, flipped, half, name):
+def product(a, weight, flipped, half, name, cost=SHORT):
     rows, tile = a.shape[0] // 2, 128
     count = rows // tile
     out = pl.BlockSpec((tile, D), lambda i, h: (i, 0))
@@ -605,46 +606,47 @@
             scratch_shapes=[pltpu.VMEM(weight.shape[::-1], bf16)] if flipped else [],
         ),
         compiler_params=pltpu.CompilerParams(vmem_limit_bytes=32 << 20),
-        cost_estimate=SHORT,
+        cost_estimate=cost,
         name=name,
     )(jnp.asarray(half, jnp.int32).reshape(1), a, a, weight)
 
 
-def finish_kernel(
-    own1_ref, sent1_ref, tok_ref, grad_ref, own2_ref, sent2_ref, resid_ref, cot_ref, vec_ref,
-    in_grad_ref, out_ref, sum_ref,
-):
-    grad = own1_ref[...] + sent1_ref[...]
-    normal, inverse = normalize(tok_ref[...].astype(f32))
-    in_grad_ref[...] = grad_ref[...] + norm_back(grad, normal, inverse, vec_ref[0:1, :])
-    mlp = own2_ref[...] + sent2_ref[...] + vec_ref[8:9, :]
-    out_ref[...] = (resid_ref[...] + vec_ref[9:10, :] * mlp).astype(bf16)
-    out_grad = cot_ref[...].astype(f32)
-
+def add_sums(sum_ref, values):
     @pl.when(pl.program_id(0) == 0)
     def _():
         sum_ref[...] = jnp.zeros_like(sum_ref)
 
-    for row, value in enumerate((grad * normal, grad, out_grad * vec_ref[9:10, :], out_grad * mlp)):
+    for row, value in enumerate(values):
         sum_ref[row : row + 1, :] += jnp.sum(value, axis=0, keepdims=True)
 
 
-def finish(own1, sent1, tok, resid_grad, own2, sent2, resid, cot, vecs):
-    rows, tile = own1.shape[0], 64
+def input_kernel(own_ref, sent_ref, tok_ref, grad_ref, vec_ref, out_ref, sum_ref):
+    grad = own_ref[...] + sent_ref[...]
+    normal, inverse = normalize(tok_ref[...].astype(f32))
+    out_ref[...] = grad_ref[...] + norm_back(grad, normal, inverse, vec_ref[0:1, :])
+    add_sums(sum_ref, (grad * normal, grad))
+
+
+def output_kernel(own_ref, sent_ref, cot_ref, resid_ref, vec_ref, out_ref, sum_ref):
+    mlp = own_ref[...] + sent_ref[...] + vec_ref[8:9, :]
+    out_ref[...] = (resid_ref[...] + vec_ref[9:10, :] * mlp).astype(bf16)
+    out_grad = cot_ref[...].astype(f32)
+    add_sums(sum_ref, (out_grad * vec_ref[9:10, :], out_grad * mlp))
+
+
+def finish(kernel, dtype, parts, vecs, name):
+    rows, tile = parts[0].shape[0], 64
     part = pl.BlockSpec((tile, D), lambda i: (i, 0))
     return pl.pallas_call(
-        finish_kernel,
-        out_shape=[
-            jax.ShapeDtypeStruct((rows, D), f32), jax.ShapeDtypeStruct((rows, D), bf16),
-            jax.ShapeDtypeStruct((8, D), f32),
-        ],
+        kernel,
+        out_shape=[jax.ShapeDtypeStruct((rows, D), dtype), jax.ShapeDtypeStruct((8, D), f32)],
         grid=(rows // tile,),
-        in_specs=[part] * 8 + [pl.BlockSpec(vecs.shape, lambda i: (0, 0))],
-        out_specs=[part, part, pl.BlockSpec((8, D), lambda i: (0, 0))],
+        in_specs=[part] * len(parts) + [pl.BlockSpec(vecs.shape, lambda i: (0, 0))],
+        out_specs=[part, pl.BlockSpec((8, D), lambda i: (0, 0))],
         compiler_params=pltpu.CompilerParams(vmem_limit_bytes=24 << 20),
         cost_estimate=SHORT,
-        name="finish",
-    )(own1, sent1, tok, resid_grad, own2, sent2, resid, cot, vecs)
+        name=name,
+    )(*parts, vecs)
 
 
 def residual_kernel(own_ref, sent_ref, tok_ref, vec_ref, attn_ref, resid_ref, input_ref):
@@ -1244,20 +1246,23 @@
     los = block_lo[own_lo:own_hi]
     los, queries = tie(los, queries)
     for pair in range(pairs):
-        if pair == 1:
+        if pair == 0:
             los, own3, *pieces2 = tie(los, own3, *pieces2)
             gather2 = Gather(pieces2, rows1, "gather2")
             los = gather2.send(los)
             pieces3 = fetch_z(own3)
-        if pair == 2:
+        if pair == 1:
             los = gather2.arrive(los)
             los = gather2.send(los)
+        if pair == 2:
+            los, *pieces3 = tie(los, *pieces3)
+            gather3 = Gather(pieces3, rows3, "gather3")
+            los = gather3.send(los)
         if pair == 3:
             los = gather2.arrive(los)
             for _ in bits[2:]:
                 los = gather2.arrive(gather2.send(los))
-            los, *pieces3 = tie(los, *pieces3)
-            gather3 = Gather(pieces3, rows3, "gather3")
+            los = gather3.arrive(los)
             los = gather3.send(los)
         context, lse = attend(
             los, block_hi[own_lo:own_hi], firsts, lasts, queries, keys, values, tag_cols,
@@ -1268,8 +1273,6 @@
         lses.append(lse)
     context = jnp.concatenate(contexts, axis=1)
     lse_rows = jnp.concatenate(lses).reshape(local_heads, chip)
-    context = gather3.arrive(context)
-    context = gather3.send(context)
     own, given = product(context, proj_matrix, False, core, "attn_out")
     attn_out, resid, mlp_input = residual(own, swap_cores(given), tok, vec_rows)
     mlp_input = jnp.concatenate([mlp_input, swap_cores(mlp_input)])
@@ -1327,10 +1330,12 @@
         )
 
     parts, sums = [], []
-    out_own, out_given = product(activated, fc2_matrix, False, 0, "mlp_out")
-    first, delta_window, lo, out_own, out_given = settle(
-        ((grads_behind[0], grads_ahead[0]), delta_window, block_lo, out_own, out_given),
-        (reduce3, "received"),
+    out_own, out_given = product(activated, fc2_matrix, False, 0, "mlp_out", FILLER)
+    output_rows, out_sums = finish(
+        output_kernel, bf16, (out_own, swap_cores(out_given), cot, resid), vec_rows, "output"
+    )
+    first, delta_window, lo, out_sums = settle(
+        ((grads_behind[0], grads_ahead[0]), delta_window, block_lo, out_sums), (reduce3, "received")
     )
     grad_windows = [jnp.concatenate([first[0], chunks[0], first[1]])]
     for pair in range(pairs):
@@ -1389,15 +1394,15 @@
         tail = reduce1b.arrive(tail)
         tail = reduce1b.send(tail)
     in_own, in_given = tail
-    input_rows, output_rows, end_sums = finish(
-        in_own, swap_cores(in_given), tok, resid_grad, out_own, swap_cores(out_given), resid, cot, vec_rows
+    input_rows, in_sums = finish(
+        input_kernel, f32, (in_own, swap_cores(in_given), tok, resid_grad), vec_rows, "input_grad"
     )
 
     vectors = (
-        end_sums[0:1], end_sums[1:2],
+        in_sums[0:1], in_sums[1:2],
         jnp.concatenate([s[0:1] for s in sums], axis=1), jnp.concatenate([s[1:2] for s in sums], axis=1),
         norm_sums[2:3], norm_sums[3:4], norm_sums[0:1], norm_sums[1:2],
-        end_sums[2:3], end_sums[3:4], fc1_bias_part,
+        out_sums[0:1], out_sums[1:2], fc1_bias_part,
     )
     of_core = [number in (2, 3, 10) for number in range(11)]
     partial = pack_grads(vectors, list(zip(sizes, of_core)), core, depth)

time: 541 us -> 542 us (level)
  starting transfers between devices: 153 us -> 132 us
  waiting for transfers between devices: 63.1 us -> 78.3 us
  Pallas kernels: 205 us -> 217 us
    ppermute x36, waiting for transfers between devices: 22 us -> 47 us  [across_rep(): return lax.ppermute(value, 'rep', [(i, i ^ 1 << bit) for i in range(size)])]
    ppermute x36, starting transfers between devices: 46 us -> 32.9 us  [across_rep(): return lax.ppermute(value, 'rep', [(i, i ^ 1 << bit) for i in range(size)])]
    ppermute x8, waiting for transfers between devices: 19.3 us -> 9.41 us  [from_chip(): return lax.ppermute(value, 'fsdp', pairs)]
    pallas_call x1 -> x2, Pallas kernels: 7.62 us -> 12.4 us  [finish(): pl.pallas_call(kernel, out_shape=[jax.ShapeDtypeStruct((rows, D), dtype),...]
    unnamed x262 -> x257, local copies, waits for them, and re-layouts: 36.5 us -> 33.1 us
  transfers between devices with their start and end apart: 80 -> 80, of which waited for: 17 -> 21; matrix products, arithmetic and copies ran while one was open for 10% -> 10% of each run, Pallas kernels for 35% -> 34%
where the time goes in v1:
time: 542 us; the launch traced here: 539 us
  Pallas kernels  217 us (40%)
  starting transfers between devices  132 us (24%)
  waiting for transfers between devices  78.3 us (14%)
  local copies, waits for them, and re-layouts  54.5 us (10%)
  other arithmetic  49.4 us (9%)
    ppermute x21, starting transfers between devices, along_z(): lax.ppermute(value, 'fsdp', [(i, (i + 2 * by) % size) for i in range(size)])  62.7 us
    pallas_call x4, Pallas kernels, attend_back(): pl.pallas_call(functools.partial(attend_back_kernel, start, stop), out_sh...  62.3 us
    pallas_call x4, Pallas kernels, attend(): pl.pallas_call(attend_kernel, out_shape=[jax.ShapeDtypeStruct((own_rows,...  47.4 us
    ppermute x36, waiting for transfers between devices, across_rep(): return lax.ppermute(value, 'rep', [(i, i ^ 1 << bit) for i in range(size)])  47 us
    ppermute x8, starting transfers between devices, from_chip(): return lax.ppermute(value, 'fsdp', pairs)  34 us
    unnamed x257, local copies, waits for them, and re-layouts  33.1 us
    ppermute x36, starting transfers between devices, across_rep(): return lax.ppermute(value, 'rep', [(i, i ^ 1 << bit) for i in range(size)])  32.9 us
    pallas_call x4, Pallas kernels, product(): pl.pallas_call(product_nt_kernel if flipped else product_kernel, out_shap...  20.3 us
  transfers between devices with their start and end apart: 80, of which 21 were waited for; matrix products, arithmetic and copies ran while one was open for 10% of the time, Pallas kernels for 34%

profile of v1, /device:TPU:0, one launch (start us, length us, event | category | flops | bytes accessed | tf_op | source)
XLA Modules:
  0.0 539.3 jit_solution(10189486604695622743)
XLA Ops:
  10.7 3.1 collective-permute-start.3
  17.7 5.8 %collective-permute-done.3.refs_1_ = bf16[272,512]{1,0:T(8,128)(2,1)} collective-permute-done((bf16[272,512]{1,0:T(8,128)(2,1)S(1)}, bf16[272,512]{1,0:T(8,128)(2,1)}, u32[]{:S(2)}, u32[]{:S(2)}) %collective-permute-start.3) | collective-permute-done | bytes 278560 | tf_op jit(solution)/shard_map/ppermute | solution.py:67
  24.9 14.0 %collective-permute-start.6 = (bf16[512,1024]{1,0:T(8,128)(2,1)S(1)}, bf16[512,1024]{1,0:T(8,128)(2,1)}, u32[]{:S(2)}, u32[]{:S(2)}) collective-permute-start(bf16[512,1024]{1,0:T(8,128)(2,1)S(1)} %bitcast.266), channel_id=1, source_target_pairs={{0,2},{1,3},{2,4},{3,5},{4,6},{5,7},{8,10},{9,11},{10,12},{11,13},... | collective-permute-start | bytes 3145736 | tf_op jit(solution)/shard_map/ppermute | solution.py:73
  49.7 7.3 %collective-permute-done.9.refs_4_ = bf16[512,1024]{1,0:T(8,128)(2,1)S(1)} collective-permute-done((bf16[512,1024]{1,0:T(8,128)(2,1)S(1)}, bf16[512,1024]{1,0:T(8,128)(2,1)S(1)}, u32[]{:S(2)}, u32[]{:S(2)}) %collective-permute-start.9) | collective-permute-done | bytes 1048608 | tf_op jit(solution)/shard_map/ppermute | solution.py:73
  66.1 7.5 %norm_window.1.n_ref = bf16[3072,1024]{1,0:T(8,128)(2,1)S(1)} custom-call(s32[12]{0:T(128)S(1)} %and_convert_fusion.need_ref, s32[2]{0:T(128)S(1)} %pad_add_fusion.1.info_ref, bf16[512,1024]{1,0:T(8,128)(2,1)} %collective-permute-done.6.refs_0_, bf16[512,1024]{1,0:T(8,128)(2,1)S(1)} %collective-permute-done.7.refs_1_, bf16[512,1024]{1,0:T(8,128)(2,1)S(1)} %bitcast.267, ...), custom_call_target="tpu_custom_call" | custom-call | flops 1 | bytes 1 | tf_op jit(solution)/shard_map/norm_window/pallas_call | solution.py:893
  73.6 7.2 %collective-permute-start.15 = (bf16[256,512]{1,0:T(8,128)(2,1)S(1)}, bf16[256,512]{1,0:T(8,128)(2,1)S(1)}, u32[]{:S(2)}, u32[]{:S(2)}) collective-permute-start(bf16[256,512]{1,0:T(8,128)(2,1)S(1)} %copy-done.93), channel_id=1, source_target_pairs={{0,2},{1,3},{2,4},{3,5},{4,6},{5,7},{6,0},{7,1},{8,10},{9,11},{10,... | collective-permute-start | bytes 786440 | tf_op jit(solution)/shard_map/ppermute | solution.py:67
  80.8 2.6 collective-permute-start.17
  88.5 8.9 %project.1 = (bf16[3072,512]{1,0:T(8,128)(2,1)S(1)}, bf16[3072,512]{1,0:T(8,128)(2,1)S(1)}, bf16[3072,512]{1,0:T(8,128)(2,1)S(1)}) custom-call(s32[12]{0:T(128)S(1)} %and_convert_fusion.need_ref, bf16[3072,1024]{1,0:T(8,128)(2,1)S(1)} %norm_window.1.n_ref, bf16[1024,1536]{1,0:T(8,128)(2,1)S(1)} %get-tuple-element.344.w_ref, f32[1,1536]{1,0:T(1,128)S(1)} %fusion.65.b_ref), custom_call_target="tpu_custom_call" | custom-call | flops 1 | bytes 1 | tf_op jit(solution)/shard_map/project/pallas_call | solution.py:845
  102.0 7.2 %collective-permute-start.20 = (bf16[512,256]{1,0:T(8,128)(2,1)S(1)}, bf16[512,256]{1,0:T(8,128)(2,1)S(1)}, u32[]{:S(2)}, u32[]{:S(2)}) collective-permute-start(bf16[512,256]{1,0:T(8,128)(2,1)S(1)} %copy-done.92), channel_id=1, source_target_pairs={{0,2},{1,3},{2,4},{3,5},{4,6},{5,7},{6,0},{7,1},{8,10},{9,11},{10,... | collective-permute-start | bytes 786440 | tf_op jit(solution)/shard_map/ppermute | solution.py:67
  110.4 3.3 collective-permute-start.22
  114.2 11.9 %attend.4 = (bf16[1024,128]{1,0:T(8,128)(2,1)S(1)}, f32[1,2,1024]{2,1,0:T(2,128)S(1)}) custom-call(s32[4]{0:T(128)S(1)} %slice.908.lo_ref, s32[4]{0:T(128)S(1)} %slice.944.hi_ref, s32[12]{0:T(128)S(1)} %convert_element_type.272.first_ref, s32[12]{0:T(128)S(1)} %convert_element_type.273.last_ref, bf16[3072,512]{1,0:T(8,128)(2,1)S(1)} %get-tuple-element.355.q_ref, ...), custom_call_target="tpu_custom_call" | custom-call | flops 1 | bytes 1 | tf_op jit(solution)/shard_map/attend/pallas_call | solution.py:972
  126.3 11.8 %attend.5 = (bf16[1024,128]{1,0:T(8,128)(2,1)S(1)}, f32[1,2,1024]{2,1,0:T(2,128)S(1)}) custom-call(s32[4]{0:T(128)S(1)} %slice.908.lo_ref, s32[4]{0:T(128)S(1)} %slice.944.hi_ref, s32[12]{0:T(128)S(1)} %convert_element_type.272.first_ref, s32[12]{0:T(128)S(1)} %convert_element_type.273.last_ref, bf16[3072,512]{1,0:T(8,128)(2,1)S(1)} %get-tuple-element.355.q_ref, ...), custom_call_target="tpu_custom_call" | custom-call | flops 1 | bytes 1 | tf_op jit(solution)/shard_map/attend/pallas_call | solution.py:972
  142.7 11.9 %attend.6 = (bf16[1024,128]{1,0:T(8,128)(2,1)S(1)}, f32[1,2,1024]{2,1,0:T(2,128)S(1)}) custom-call(s32[4]{0:T(128)S(1)} %slice.908.lo_ref, s32[4]{0:T(128)S(1)} %slice.944.hi_ref, s32[12]{0:T(128)S(1)} %convert_element_type.272.first_ref, s32[12]{0:T(128)S(1)} %convert_element_type.273.last_ref, bf16[3072,512]{1,0:T(8,128)(2,1)S(1)} %get-tuple-element.355.q_ref, ...), custom_call_target="tpu_custom_call" | custom-call | flops 1 | bytes 1 | tf_op jit(solution)/shard_map/attend/pallas_call | solution.py:972
  154.7 9.6 %collective-permute-done.23.refs_1_ = bf16[2,4,128,512]{3,2,1,0:T(8,128)(2,1)S(1)} collective-permute-done((bf16[2,4,128,512]{3,2,1,0:T(8,128)(2,1)S(1)}, bf16[2,4,128,512]{3,2,1,0:T(8,128)(2,1)S(1)}, u32[]{:S(2)}, u32[]{:S(2)}) %collective-permute-start.23) | collective-permute-done | bytes 1048608 | tf_op jit(solution)/shard_map/ppermute | solution.py:78
  164.4 8.3 %collective-permute-done.25 = bf16[1,4,256,256]{3,2,1,0:T(8,128)(2,1)S(1)} collective-permute-done((bf16[1,4,256,256]{3,2,1,0:T(8,128)(2,1)S(1)}, bf16[1,4,256,256]{3,2,1,0:T(8,128)(2,1)S(1)}, u32[]{:S(2)}, u32[]{:S(2)}) %collective-permute-start.25) | collective-permute-done | bytes 524320 | tf_op jit(solution)/shard_map/ppermute | solution.py:78
  173.0 11.9 %attend.7 = (bf16[1024,128]{1,0:T(8,128)(2,1)S(1)}, f32[1,2,1024]{2,1,0:T(2,128)S(1)}) custom-call(s32[4]{0:T(128)S(1)} %slice.908.lo_ref, s32[4]{0:T(128)S(1)} %slice.944.hi_ref, s32[12]{0:T(128)S(1)} %convert_element_type.272.first_ref, s32[12]{0:T(128)S(1)} %convert_element_type.273.last_ref, bf16[3072,512]{1,0:T(8,128)(2,1)S(1)} %get-tuple-element.355.q_ref, ...), custom_call_target="tpu_custom_call" | custom-call | flops 1 | bytes 1 | tf_op jit(solution)/shard_map/attend/pallas_call | solution.py:972
  187.4 3.6 collective-permute-done.27.sent_ref
  197.5 9.6 %units.1 = (bf16[1024,2048]{1,0:T(8,128)(2,1)S(1)}, bf16[1024,2048]{1,0:T(8,128)(2,1)S(1)}) custom-call(bf16[1024,1024]{1,0:T(8,128)(2,1)S(1)} %constant_dynamic-update-slice_fusion.4.n_ref.a_ref, bf16[1024,2048]{1,0:T(8,128)(2,1)S(1)} %gather2.1.w_ref, f32[1,2048]{1,0:T(1,128)S(1)} %copy-done.74), custom_call_target="tpu_custom_call" | custom-call | flops 1 | bytes 1 | tf_op jit(solution)/shard_map/units/pallas_call | solution.py:702
  211.2 7.5 %collective-permute-done.29.refs_1_ = bf16[2,4,256,256]{3,2,1,0:T(8,128)(2,1)S(1)} collective-permute-done((bf16[2,4,256,256]{3,2,1,0:T(8,128)(2,1)S(1)}, bf16[2,4,256,256]{3,2,1,0:T(8,128)(2,1)S(1)}, u32[]{:S(2)}, u32[]{:S(2)}) %collective-permute-start.29) | collective-permute-done | bytes 1048608 | tf_op jit(solution)/shard_map/ppermute | solution.py:78
  221.8 7.0 %fc2_grad.1 = (bf16[2,4,256,256]{3,2,1,0:T(8,128)(2,1)S(1)}, bf16[2,4,256,256]{3,2,1,0:T(8,128)(2,1)}, bf16[2,4,256,256]{3,2,1,0:T(8,128)(2,1)S(1)}, bf16[2,4,256,256]{3,2,1,0:T(8,128)(2,1)}) custom-call(s32[1]{0:T(128)} %bitcast.3.index_ref, bf16[1024,2048]{1,0:T(8,128)(2,1)S(1)} %copy-done.30, bf16[1024,1024]{1,0:T(8,128)(2,1)S(1)} %scaled.1.b_ref.g_ref), custom_call_target="tpu_custom_call" | custom-call | flops 1 | bytes 1 | tf_op jit(solution)/shard_map/fc2_grad/pallas_call | solution.py:531
  231.9 8.9 %pre_grad.1 = (bf16[1024,2048]{1,0:T(8,128)(2,1)S(1)}, f32[1,2048]{1,0:T(1,128)S(1)}) custom-call(bf16[1024,1024]{1,0:T(8,128)(2,1)S(1)} %scaled.1.b_ref.g_ref, bf16[2048,1024]{1,0:T(8,128)(2,1)S(1)} %gather3.1.w_ref, bf16[1024,2048]{1,0:T(8,128)(2,1)} %copy-done.32), custom_call_target="tpu_custom_call" | custom-call | flops 1 | bytes 1 | tf_op jit(solution)/shard_map/pre_grad/pallas_call | solution.py:560
  240.8 6.8 %fc1_grad.1 = (bf16[2,4,128,512]{3,2,1,0:T(8,128)(2,1)S(1)}, bf16[2,4,128,512]{3,2,1,0:T(8,128)(2,1)}, bf16[2,4,128,512]{3,2,1,0:T(8,128)(2,1)S(1)}, bf16[2,4,128,512]{3,2,1,0:T(8,128)(2,1)}) custom-call(s32[1]{0:T(128)} %bitcast.3.index_ref, bf16[1024,1024]{1,0:T(8,128)(2,1)S(1)} %copy-done.15, ...), custom_call_target="tpu_custom_call" | custom-call | flops 1 | bytes 1 | tf_op jit(solution)/shard_map/fc1_grad/pallas_call | solution.py:531
  247.7 6.6 %mlp_in_grad.1 = (f32[512,1024]{1,0:T(8,128)S(1)}, f32[512,1024]{1,0:T(8,128)S(1)}) custom-call(s32[1]{0:T(128)} %constant.138.clone.1.half_ref, bf16[1024,2048]{1,0:T(8,128)(2,1)S(1)} %get-tuple-element.419.b_ref.first_ref.second_ref, bf16[1024,2048]{1,0:T(8,128)(2,1)S(1)} %get-tuple-element.419.b_ref.first_ref.second_ref, bf16[1024,2048]{1,0:T(8,128)(2,1)S(1)} %gather2.1.w_ref), custom_call_target="tpu_custom_call" | custom-call | flops 1 | bytes 1 | tf_op jit(solution)/shard_map/mlp_in_grad/pallas_call | solution.py:594
  260.5 4.2 collective-permute-done.33.sent_ref
  264.7 4.5 norm_grad.1
  279.6 5.9 %mlp_out.1 = (f32[512,1024]{1,0:T(8,128)S(1)}, f32[512,1024]{1,0:T(8,128)}) custom-call(s32[1]{0:T(128)} %constant.138.clone.1.half_ref, bf16[1024,2048]{1,0:T(8,128)(2,1)S(1)} %copy-done.31, bf16[1024,2048]{1,0:T(8,128)(2,1)S(1)} %copy-done.31, bf16[2048,1024]{1,0:T(8,128)(2,1)S(1)} %copy-done.12), custom_call_target="tpu_custom_call" | custom-call | flops 8589934592 | bytes 8388608 | tf_op jit(solution)/shard_map/mlp_out/pallas_call | solution.py:594
  289.9 2.8 fusion
  292.7 6.2 %collective-permute-start.38 = (f32[16,1024]{1,0:T(8,128)S(1)}, f32[16,1024]{1,0:T(8,128)S(1)}, u32[]{:S(2)}, u32[]{:S(2)}) collective-permute-start(f32[16,1024]{1,0:T(8,128)S(1)} %pad_maximum_fusion.24), channel_id=1, source_target_pairs={{0,2},{1,3},{2,4},{3,5},{4,6},{5,7},{8,10},{9,11},{10,12},{11,13},... | collective-permute-start | bytes 196616 | tf_op jit(solution)/shard_map/ppermute | solution.py:73
  301.2 5.3 collective-permute-start.36
  314.0 5.6 %output.1 = (bf16[512,1024]{1,0:T(8,128)(2,1)}, f32[8,1024]{1,0:T(8,128)S(1)}) custom-call(f32[512,1024]{1,0:T(8,128)S(1)} %copy-done.39, f32[512,1024]{1,0:T(8,128)} %collective-permute-done.35.sent_ref, bf16[512,1024]{1,0:T(8,128)(2,1)S(1)} %bitcast.263, f32[512,1024]{1,0:T(8,128)S(1)} %copy-done.26, f32[16,1024]{1,0:T(8,128)S(1)} %copy-done.33), custom_call_target="tpu_custom_call" | custom-call | flops 1 | bytes 1 | tf_op jit(solution)/shard_map/output/pallas_call | solution.py:640
  323.6 3.4 collective-permute-start.42
  334.3 15.6 %attend_back.4 = (bf16[1024,128]{1,0:T(8,128)(2,1)S(1)}, bf16[1024,128]{1,0:T(8,128)(2,1)S(1)}, bf16[1024,128]{1,0:T(8,128)(2,1)S(1)}, f32[1,8,128]{2,1,0:T(8,128)S(1)}) custom-call(s32[12]{0:T(128)S(1)} %get-tuple-element.540.lo_ref, s32[12]{0:T(128)S(1)} %get-tuple-element.829.hi_ref, bf16[3072,512]{1,0:T(8,128)(2,1)S(1)} %get-tuple-element.355.q_ref, ...), custom_call_target="tpu_custom_call" | custom-call | flops 1 | bytes 1 | tf_op jit(solution)/shard_map/attend_back/pallas_call | solution.py:1082
  359.2 6.1 %collective-permute-start.48 = (bf16[512,256]{1,0:T(8,128)(2,1)}, bf16[512,256]{1,0:T(8,128)(2,1)}, u32[]{:S(2)}, u32[]{:S(2)}) collective-permute-start(bf16[512,256]{1,0:T(8,128)(2,1)} %get-tuple-element.482), channel_id=1, source_target_pairs={{0,2},{1,3},{2,4},{3,5},{4,6},{5,7},{6,0},{7,1},{8,10},{9,11},{10,... | collective-permute-start | bytes 786440 | tf_op jit(solution)/shard_map/ppermute | solution.py:67
  365.3 2.8 collective-permute-start.50
  369.5 15.4 %attend_back.5 = (bf16[1024,128]{1,0:T(8,128)(2,1)S(1)}, bf16[1024,128]{1,0:T(8,128)(2,1)S(1)}, bf16[1024,128]{1,0:T(8,128)(2,1)S(1)}, f32[1,8,128]{2,1,0:T(8,128)S(1)}) custom-call(s32[12]{0:T(128)S(1)} %get-tuple-element.540.lo_ref, s32[12]{0:T(128)S(1)} %get-tuple-element.829.hi_ref, bf16[3072,512]{1,0:T(8,128)(2,1)S(1)} %get-tuple-element.355.q_ref, ...), custom_call_target="tpu_custom_call" | custom-call | flops 1 | bytes 1 | tf_op jit(solution)/shard_map/attend_back/pallas_call | solution.py:1082
  393.8 4.9 collective-permute-start.51
  400.7 2.9 collective-permute-start.53
  404.9 15.8 %attend_back.6 = (bf16[1024,128]{1,0:T(8,128)(2,1)S(1)}, bf16[1024,128]{1,0:T(8,128)(2,1)S(1)}, bf16[1024,128]{1,0:T(8,128)(2,1)S(1)}, f32[1,8,128]{2,1,0:T(8,128)S(1)}) custom-call(s32[12]{0:T(128)S(1)} %get-tuple-element.540.lo_ref, s32[12]{0:T(128)S(1)} %get-tuple-element.829.hi_ref, bf16[3072,512]{1,0:T(8,128)(2,1)S(1)} %get-tuple-element.355.q_ref, ...), custom_call_target="tpu_custom_call" | custom-call | flops 1 | bytes 1 | tf_op jit(solution)/shard_map/attend_back/pallas_call | solution.py:1082
  431.0 15.4 %attend_back.7 = (bf16[1024,128]{1,0:T(8,128)(2,1)S(1)}, bf16[1024,128]{1,0:T(8,128)(2,1)S(1)}, bf16[1024,128]{1,0:T(8,128)(2,1)S(1)}, f32[1,8,128]{2,1,0:T(8,128)S(1)}) custom-call(s32[12]{0:T(128)S(1)} %get-tuple-element.540.lo_ref, s32[12]{0:T(128)S(1)} %get-tuple-element.829.hi_ref, bf16[3072,512]{1,0:T(8,128)(2,1)S(1)} %get-tuple-element.355.q_ref, ...), custom_call_target="tpu_custom_call" | custom-call | flops 1 | bytes 1 | tf_op jit(solution)/shard_map/attend_back/pallas_call | solution.py:1082
  454.3 7.7 %collective-permute-start.62 = (bf16[256,256]{1,0:T(8,128)(2,1)S(1)}, bf16[256,256]{1,0:T(8,128)(2,1)S(1)}, u32[]{:S(2)}, u32[]{:S(2)}) collective-permute-start(bf16[256,256]{1,0:T(8,128)(2,1)S(1)} %get-tuple-element.574), channel_id=1, source_target_pairs={{0,2},{1,3},{2,4},{3,5},{4,6},{5,7},{6,0},{7,1},{8,10},{9,11},{10,... | collective-permute-start | bytes 393224 | tf_op jit(solution)/shard_map/ppermute | solution.py:67
  462.8 2.9 collective-permute-start.64
  466.1 6.1 %attn_in_grad.1 = (f32[512,1024]{1,0:T(8,128)S(1)}, f32[512,1024]{1,0:T(8,128)}) custom-call(s32[1]{0:T(128)} %bitcast.2.half_ref.index_ref, bf16[1024,1536]{1,0:T(8,128)(2,1)S(1)} %constant_dynamic-update-slice_fusion.6.first_ref.second_ref, bf16[1024,1536]{1,0:T(8,128)(2,1)S(1)} %constant_dynamic-update-slice_fusion.6.first_ref.second_ref, ...), custom_call_target="tpu_custom_call" | custom-call | flops 1 | bytes 1 | tf_op jit(solution)/shard_map/attn_in_grad/pallas_call | solution.py:594
  482.3 6.8 %input_grad.1 = (f32[512,1024]{1,0:T(8,128)}, f32[8,1024]{1,0:T(8,128)S(1)}) custom-call(f32[512,1024]{1,0:T(8,128)S(1)} %copy-done.37, f32[512,1024]{1,0:T(8,128)} %collective-permute-done.65.sent_ref, bf16[512,1024]{1,0:T(8,128)(2,1)S(1)} %bitcast.269, f32[512,1024]{1,0:T(8,128)S(1)} %copy-done.35, f32[16,1024]{1,0:T(8,128)S(1)} %copy-done.33), custom_call_target="tpu_custom_call" | custom-call | flops 1 | bytes 1 | tf_op jit(solution)/shard_map/input_grad/pallas_call | solution.py:640
  493.9 4.2 collective-permute-done.67
  508.8 4.7 collective-permute-done.70
  516.5 2.9 collective-permute-done.75
  523.5 4.1 collective-permute-done.77
  527.8 4.8 collective-permute-done.76
  (578 shorter events, 192.4 us)
Async XLA Ops:
  13.8 52.3 %collective-permute-start.8 = (bf16[512,1024]{1,0:T(8,128)(2,1)S(1)}, bf16[512,1024]{1,0:T(8,128)(2,1)S(1)}, u32[]{:S(2)}, u32[]{:S(2)}) collective-permute-start(bf16[512,1024]{1,0:T(8,128)(2,1)S(1)} %bitcast.264), channel_id=1, source_target_pairs={{0,1},{1,0},{2,3},{3,2},{4,5},{5,4},{6,7},{7,6},{8,9},{9,8},{10,11... | collective-permute-start | bytes 3145736 | tf_op jit(solution)/shard_map/ppermute | solution.py:62
  13.8 26.0 %collective-permute-start.4 = (bf16[272,512]{1,0:T(8,128)(2,1)S(1)}, bf16[272,512]{1,0:T(8,128)(2,1)S(1)}, u32[]{:S(2)}, u32[]{:S(2)}) collective-permute-start(bf16[272,512]{1,0:T(8,128)(2,1)S(1)} %pad_maximum_fusion.16.refs_0_), channel_id=1, source_target_pairs={{0,4},{1,5},{2,6},{3,7},{4,0},{5,1},{6,2},{7,3},{8,12},{9,13},{10,... | collective-permute-start | bytes 835592 | tf_op jit(solution)/shard_map/ppermute | solution.py:67
  16.4 23.5 %collective-permute-start.5 = (bf16[272,512]{1,0:T(8,128)(2,1)S(1)}, bf16[272,512]{1,0:T(8,128)(2,1)S(1)}, u32[]{:S(2)}, u32[]{:S(2)}) collective-permute-start(bf16[272,512]{1,0:T(8,128)(2,1)S(1)} %pad_maximum_fusion.16.refs_0_), channel_id=1, source_target_pairs={{0,6},{1,7},{2,0},{3,1},{4,2},{5,3},{6,4},{7,5},{8,14},{9,15},{10,... | collective-permute-start | bytes 835592 | tf_op jit(solution)/shard_map/ppermute | solution.py:67
  23.6 33.5 %collective-permute-start.9 = (bf16[512,1024]{1,0:T(8,128)(2,1)S(1)}, bf16[512,1024]{1,0:T(8,128)(2,1)S(1)}, u32[]{:S(2)}, u32[]{:S(2)}) collective-permute-start(bf16[512,1024]{1,0:T(8,128)(2,1)S(1)} %bitcast.265), channel_id=1, source_target_pairs={{2,0},{3,1},{4,2},{5,3},{6,4},{7,5},{10,8},{11,9},{12,10},{13,11},... | collective-permute-start | bytes 3145736 | tf_op jit(solution)/shard_map/ppermute | solution.py:73
  24.9 32.2 %collective-permute-start.6 = (bf16[512,1024]{1,0:T(8,128)(2,1)S(1)}, bf16[512,1024]{1,0:T(8,128)(2,1)}, u32[]{:S(2)}, u32[]{:S(2)}) collective-permute-start(bf16[512,1024]{1,0:T(8,128)(2,1)S(1)} %bitcast.266), channel_id=1, source_target_pairs={{0,2},{1,3},{2,4},{3,5},{4,6},{5,7},{8,10},{9,11},{10,12},{11,13},... | collective-permute-start | bytes 3145736 | tf_op jit(solution)/shard_map/ppermute | solution.py:73
  60.2 25.1 %collective-permute-start.13 = (bf16[2,4,128,512]{3,2,1,0:T(8,128)(2,1)S(1)}, bf16[2,4,128,512]{3,2,1,0:T(8,128)(2,1)S(1)}, u32[]{:S(2)}, u32[]{:S(2)}) collective-permute-start(bf16[2,4,128,512]{3,2,1,0:T(8,128)(2,1)S(1)} %pad_maximum_fusion.2.refs_0_), channel_id=1, source_target_pairs={{0,16},{8,24},{16,0},{24,8},{1,17},{9,25},{17,1},{25,9},{2,18},{10... | collective-permute-start | bytes 3145736 | tf_op jit(solution)/shard_map/ppermute | solution.py:78
  61.8 24.8 %collective-permute-start.14 = (bf16[2,4,128,512]{3,2,1,0:T(8,128)(2,1)S(1)}, bf16[2,4,128,512]{3,2,1,0:T(8,128)(2,1)S(1)}, u32[]{:S(2)}, u32[]{:S(2)}) collective-permute-start(bf16[2,4,128,512]{3,2,1,0:T(8,128)(2,1)S(1)} %pad_maximum_fusion.3.refs_2_), channel_id=1, source_target_pairs={{0,8},{8,0},{16,24},{24,16},{1,9},{9,1},{17,25},{25,17},{2,10},{10... | collective-permute-start | bytes 3145736 | tf_op jit(solution)/shard_map/ppermute | solution.py:78
  73.6 26.4 %collective-permute-start.15 = (bf16[256,512]{1,0:T(8,128)(2,1)S(1)}, bf16[256,512]{1,0:T(8,128)(2,1)S(1)}, u32[]{:S(2)}, u32[]{:S(2)}) collective-permute-start(bf16[256,512]{1,0:T(8,128)(2,1)S(1)} %copy-done.93), channel_id=1, source_target_pairs={{0,2},{1,3},{2,4},{3,5},{4,6},{5,7},{6,0},{7,1},{8,10},{9,11},{10,... | collective-permute-start | bytes 786440 | tf_op jit(solution)/shard_map/ppermute | solution.py:67
  80.8 19.3 %collective-permute-start.16 = (bf16[256,512]{1,0:T(8,128)(2,1)S(1)}, bf16[256,512]{1,0:T(8,128)(2,1)S(1)}, u32[]{:S(2)}, u32[]{:S(2)}) collective-permute-start(bf16[256,512]{1,0:T(8,128)(2,1)S(1)} %copy-done.93), channel_id=1, source_target_pairs={{0,4},{1,5},{2,6},{3,7},{4,0},{5,1},{6,2},{7,3},{8,12},{9,13},{10,... | collective-permute-start | bytes 786440 | tf_op jit(solution)/shard_map/ppermute | solution.py:67
  80.8 19.3 %collective-permute-start.17 = (bf16[256,512]{1,0:T(8,128)(2,1)S(1)}, bf16[256,512]{1,0:T(8,128)(2,1)S(1)}, u32[]{:S(2)}, u32[]{:S(2)}) collective-permute-start(bf16[256,512]{1,0:T(8,128)(2,1)S(1)} %copy-done.93), channel_id=1, source_target_pairs={{0,6},{1,7},{2,0},{3,1},{4,2},{5,3},{6,4},{7,5},{8,14},{9,15},{10,... | collective-permute-start | bytes 786440 | tf_op jit(solution)/shard_map/ppermute | solution.py:67
  100.3 25.7 %collective-permute-start.18 = (bf16[1,4,128,512]{3,2,1,0:T(8,128)(2,1)S(1)}, bf16[1,4,128,512]{3,2,1,0:T(8,128)(2,1)S(1)}, u32[]{:S(2)}, u32[]{:S(2)}) collective-permute-start(bf16[1,4,128,512]{3,2,1,0:T(8,128)(2,1)S(1)} %maximum_bitcast_fusion.2), channel_id=1, source_target_pairs={{0,8},{8,0},{16,24},{24,16},{1,9},{9,1},{17,25},{25,17},{2,10},{10... | collective-permute-start | bytes 1572872 | tf_op jit(solution)/shard_map/ppermute | solution.py:78
  101.9 24.2 %collective-permute-start.19 = (bf16[1,4,128,512]{3,2,1,0:T(8,128)(2,1)S(1)}, bf16[1,4,128,512]{3,2,1,0:T(8,128)(2,1)S(1)}, u32[]{:S(2)}, u32[]{:S(2)}) collective-permute-start(bf16[1,4,128,512]{3,2,1,0:T(8,128)(2,1)S(1)} %maximum_bitcast_fusion.3), channel_id=1, source_target_pairs={{0,16},{8,24},{16,0},{24,8},{1,17},{9,25},{17,1},{25,9},{2,18},{10... | collective-permute-start | bytes 1572872 | tf_op jit(solution)/shard_map/ppermute | solution.py:78
  102.0 36.2 %collective-permute-start.20 = (bf16[512,256]{1,0:T(8,128)(2,1)S(1)}, bf16[512,256]{1,0:T(8,128)(2,1)S(1)}, u32[]{:S(2)}, u32[]{:S(2)}) collective-permute-start(bf16[512,256]{1,0:T(8,128)(2,1)S(1)} %copy-done.92), channel_id=1, source_target_pairs={{0,2},{1,3},{2,4},{3,5},{4,6},{5,7},{6,0},{7,1},{8,10},{9,11},{10,... | collective-permute-start | bytes 786440 | tf_op jit(solution)/shard_map/ppermute | solution.py:67
  109.2 29.0 %collective-permute-start.21 = (bf16[512,256]{1,0:T(8,128)(2,1)S(1)}, bf16[512,256]{1,0:T(8,128)(2,1)S(1)}, u32[]{:S(2)}, u32[]{:S(2)}) collective-permute-start(bf16[512,256]{1,0:T(8,128)(2,1)S(1)} %copy-done.92), channel_id=1, source_target_pairs={{0,4},{1,5},{2,6},{3,7},{4,0},{5,1},{6,2},{7,3},{8,12},{9,13},{10,... | collective-permute-start | bytes 786440 | tf_op jit(solution)/shard_map/ppermute | solution.py:67
  110.4 27.8 %collective-permute-start.22 = (bf16[512,256]{1,0:T(8,128)(2,1)S(1)}, bf16[512,256]{1,0:T(8,128)(2,1)S(1)}, u32[]{:S(2)}, u32[]{:S(2)}) collective-permute-start(bf16[512,256]{1,0:T(8,128)(2,1)S(1)} %copy-done.92), channel_id=1, source_target_pairs={{0,6},{1,7},{2,0},{3,1},{4,2},{5,3},{6,4},{7,5},{8,14},{9,15},{10,... | collective-permute-start | bytes 786440 | tf_op jit(solution)/shard_map/ppermute | solution.py:67
  138.2 26.1 %collective-permute-start.23 = (bf16[2,4,128,512]{3,2,1,0:T(8,128)(2,1)S(1)}, bf16[2,4,128,512]{3,2,1,0:T(8,128)(2,1)S(1)}, u32[]{:S(2)}, u32[]{:S(2)}) collective-permute-start(bf16[2,4,128,512]{3,2,1,0:T(8,128)(2,1)S(1)} %pad_maximum_fusion.4.refs_0_), channel_id=1, source_target_pairs={{0,16},{8,24},{16,0},{24,8},{1,17},{9,25},{17,1},{25,9},{2,18},{10... | collective-permute-start | bytes 3145736 | tf_op jit(solution)/shard_map/ppermute | solution.py:78
  138.3 26.1 %collective-permute-start.24 = (bf16[2,4,128,512]{3,2,1,0:T(8,128)(2,1)S(1)}, bf16[2,4,128,512]{3,2,1,0:T(8,128)(2,1)S(1)}, u32[]{:S(2)}, u32[]{:S(2)}) collective-permute-start(bf16[2,4,128,512]{3,2,1,0:T(8,128)(2,1)S(1)} %pad_maximum_fusion.5.refs_2_), channel_id=1, source_target_pairs={{0,8},{8,0},{16,24},{24,16},{1,9},{9,1},{17,25},{25,17},{2,10},{10... | collective-permute-start | bytes 3145736 | tf_op jit(solution)/shard_map/ppermute | solution.py:78
  138.7 34.0 %collective-permute-start.25 = (bf16[1,4,256,256]{3,2,1,0:T(8,128)(2,1)S(1)}, bf16[1,4,256,256]{3,2,1,0:T(8,128)(2,1)S(1)}, u32[]{:S(2)}, u32[]{:S(2)}) collective-permute-start(bf16[1,4,256,256]{3,2,1,0:T(8,128)(2,1)S(1)} %maximum_bitcast_fusion.4), channel_id=1, source_target_pairs={{0,8},{8,0},{16,24},{24,16},{1,9},{9,1},{17,25},{25,17},{2,10},{10... | collective-permute-start | bytes 1572872 | tf_op jit(solution)/shard_map/ppermute | solution.py:78
  140.7 32.0 %collective-permute-start.26 = (bf16[1,4,256,256]{3,2,1,0:T(8,128)(2,1)S(1)}, bf16[1,4,256,256]{3,2,1,0:T(8,128)(2,1)S(1)}, u32[]{:S(2)}, u32[]{:S(2)}) collective-permute-start(bf16[1,4,256,256]{3,2,1,0:T(8,128)(2,1)S(1)} %maximum_bitcast_fusion.5), channel_id=1, source_target_pairs={{0,16},{8,24},{16,0},{24,8},{1,17},{9,25},{17,1},{25,9},{2,18},{10... | collective-permute-start | bytes 1572872 | tf_op jit(solution)/shard_map/ppermute | solution.py:78
  193.3 25.4 %collective-permute-start.29 = (bf16[2,4,256,256]{3,2,1,0:T(8,128)(2,1)S(1)}, bf16[2,4,256,256]{3,2,1,0:T(8,128)(2,1)S(1)}, u32[]{:S(2)}, u32[]{:S(2)}) collective-permute-start(bf16[2,4,256,256]{3,2,1,0:T(8,128)(2,1)S(1)} %pad_maximum_fusion.6.refs_0_), channel_id=1, source_target_pairs={{0,16},{8,24},{16,0},{24,8},{1,17},{9,25},{17,1},{25,9},{2,18},{10... | collective-permute-start | bytes 3145736 | tf_op jit(solution)/shard_map/ppermute | solution.py:78
  194.5 25.2 %collective-permute-start.30 = (bf16[2,4,256,256]{3,2,1,0:T(8,128)(2,1)S(1)}, bf16[2,4,256,256]{3,2,1,0:T(8,128)(2,1)S(1)}, u32[]{:S(2)}, u32[]{:S(2)}) collective-permute-start(bf16[2,4,256,256]{3,2,1,0:T(8,128)(2,1)S(1)} %pad_maximum_fusion.7.refs_2_), channel_id=1, source_target_pairs={{0,8},{8,0},{16,24},{24,16},{1,9},{9,1},{17,25},{25,17},{2,10},{10... | collective-permute-start | bytes 3145736 | tf_op jit(solution)/shard_map/ppermute | solution.py:78
  228.8 25.4 %collective-permute-start.31 = (bf16[2,4,256,256]{3,2,1,0:T(8,128)(2,1)}, bf16[2,4,256,256]{3,2,1,0:T(8,128)(2,1)}, u32[]{:S(2)}, u32[]{:S(2)}) collective-permute-start(bf16[2,4,256,256]{3,2,1,0:T(8,128)(2,1)} %get-tuple-element.422), channel_id=1, source_target_pairs={{0,8},{8,0},{16,24},{24,16},{1,9},{9,1},{17,25},{25,17},{2,10},{10... | collective-permute-start | bytes 3145736 | tf_op jit(solution)/shard_map/ppermute | solution.py:78
  229.1 25.2 %collective-permute-start.32 = (bf16[2,4,256,256]{3,2,1,0:T(8,128)(2,1)}, bf16[2,4,256,256]{3,2,1,0:T(8,128)(2,1)}, u32[]{:S(2)}, u32[]{:S(2)}) collective-permute-start(bf16[2,4,256,256]{3,2,1,0:T(8,128)(2,1)} %get-tuple-element.423), channel_id=1, source_target_pairs={{0,16},{8,24},{16,0},{24,8},{1,17},{9,25},{17,1},{25,9},{2,18},{10... | collective-permute-start | bytes 3145736 | tf_op jit(solution)/shard_map/ppermute | solution.py:78
  286.7 22.8 %collective-permute-start.35 = (f32[512,1024]{1,0:T(8,128)}, f32[512,1024]{1,0:T(8,128)}, u32[]{:S(2)}, u32[]{:S(2)}) collective-permute-start(f32[512,1024]{1,0:T(8,128)} %get-tuple-element.437), channel_id=1, source_target_pairs={{0,1},{1,0},{2,3},{3,2},{4,5},{5,4},{6,7},{7,6},{8,9},{9,8},{10,11... | collective-permute-start | bytes 6291464 | tf_op jit(solution)/shard_map/ppermute | solution.py:62
  287.0 32.6 %collective-permute-start.40 = (bf16[1,4,256,256]{3,2,1,0:T(8,128)(2,1)}, bf16[1,4,256,256]{3,2,1,0:T(8,128)(2,1)}, u32[]{:S(2)}, u32[]{:S(2)}) collective-permute-start(bf16[1,4,256,256]{3,2,1,0:T(8,128)(2,1)} %slice.1111), channel_id=1, source_target_pairs={{0,16},{8,24},{16,0},{24,8},{1,17},{9,25},{17,1},{25,9},{2,18},{10... | collective-permute-start | bytes 1572872 | tf_op jit(solution)/shard_map/ppermute | solution.py:78
  288.2 31.4 %collective-permute-start.41 = (bf16[1,4,256,256]{3,2,1,0:T(8,128)(2,1)}, bf16[1,4,256,256]{3,2,1,0:T(8,128)(2,1)}, u32[]{:S(2)}, u32[]{:S(2)}) collective-permute-start(bf16[1,4,256,256]{3,2,1,0:T(8,128)(2,1)} %slice.1112), channel_id=1, source_target_pairs={{0,8},{8,0},{16,24},{24,16},{1,9},{9,1},{17,25},{25,17},{2,10},{10... | collective-permute-start | bytes 1572872 | tf_op jit(solution)/shard_map/ppermute | solution.py:78
  301.2 18.3 %collective-permute-start.36 = (bf16[1024,256]{1,0:T(8,128)(2,1)}, bf16[1024,256]{1,0:T(8,128)(2,1)}, u32[]{:S(2)}, u32[]{:S(2)}) collective-permute-start(bf16[1024,256]{1,0:T(8,128)(2,1)} %get-tuple-element.674), channel_id=1, source_target_pairs={{0,2},{1,3},{2,4},{3,5},{4,6},{5,7},{8,10},{9,11},{10,12},{11,13},... | collective-permute-start | bytes 1572872 | tf_op jit(solution)/shard_map/ppermute | solution.py:73
  321.6 30.7 %collective-permute-start.44 = (bf16[2,4,128,512]{3,2,1,0:T(8,128)(2,1)}, bf16[2,4,128,512]{3,2,1,0:T(8,128)(2,1)}, u32[]{:S(2)}, u32[]{:S(2)}) collective-permute-start(bf16[2,4,128,512]{3,2,1,0:T(8,128)(2,1)} %get-tuple-element.460), channel_id=1, source_target_pairs={{0,8},{8,0},{16,24},{24,16},{1,9},{9,1},{17,25},{25,17},{2,10},{10... | collective-permute-start | bytes 3145736 | tf_op jit(solution)/shard_map/ppermute | solution.py:78
  322.7 29.6 %collective-permute-start.45 = (bf16[2,4,128,512]{3,2,1,0:T(8,128)(2,1)}, bf16[2,4,128,512]{3,2,1,0:T(8,128)(2,1)}, u32[]{:S(2)}, u32[]{:S(2)}) collective-permute-start(bf16[2,4,128,512]{3,2,1,0:T(8,128)(2,1)} %get-tuple-element.461), channel_id=1, source_target_pairs={{0,16},{8,24},{16,0},{24,8},{1,17},{9,25},{17,1},{25,9},{2,18},{10... | collective-permute-start | bytes 3145736 | tf_op jit(solution)/shard_map/ppermute | solution.py:78
  323.6 28.7 %collective-permute-start.42 = (bf16[1024,256]{1,0:T(8,128)(2,1)}, bf16[1024,256]{1,0:T(8,128)(2,1)}, u32[]{:S(2)}, u32[]{:S(2)}) collective-permute-start(bf16[1024,256]{1,0:T(8,128)(2,1)} %get-tuple-element.673), channel_id=1, source_target_pairs={{0,2},{1,3},{2,4},{3,5},{4,6},{5,7},{8,10},{9,11},{10,12},{11,13},... | collective-permute-start | bytes 1572872 | tf_op jit(solution)/shard_map/ppermute | solution.py:73
  327.0 25.3 %collective-permute-start.43 = (bf16[1024,256]{1,0:T(8,128)(2,1)}, bf16[1024,256]{1,0:T(8,128)(2,1)}, u32[]{:S(2)}, u32[]{:S(2)}) collective-permute-start(bf16[1024,256]{1,0:T(8,128)(2,1)} %get-tuple-element.673), channel_id=1, source_target_pairs={{2,0},{3,1},{4,2},{5,3},{6,4},{7,5},{10,8},{11,9},{12,10},{13,11},... | collective-permute-start | bytes 1572872 | tf_op jit(solution)/shard_map/ppermute | solution.py:73
  357.5 29.7 %collective-permute-start.46 = (bf16[1,4,128,512]{3,2,1,0:T(8,128)(2,1)}, bf16[1,4,128,512]{3,2,1,0:T(8,128)(2,1)S(1)}, u32[]{:S(2)}, u32[]{:S(2)}) collective-permute-start(bf16[1,4,128,512]{3,2,1,0:T(8,128)(2,1)} %slice.1117), channel_id=1, source_target_pairs={{0,16},{8,24},{16,0},{24,8},{1,17},{9,25},{17,1},{25,9},{2,18},{10... | collective-permute-start | bytes 1572872 | tf_op jit(solution)/shard_map/ppermute | solution.py:78
  357.5 29.7 %collective-permute-start.47 = (bf16[1,4,128,512]{3,2,1,0:T(8,128)(2,1)}, bf16[1,4,128,512]{3,2,1,0:T(8,128)(2,1)}, u32[]{:S(2)}, u32[]{:S(2)}) collective-permute-start(bf16[1,4,128,512]{3,2,1,0:T(8,128)(2,1)} %slice.1118), channel_id=1, source_target_pairs={{0,8},{8,0},{16,24},{24,16},{1,9},{9,1},{17,25},{25,17},{2,10},{10... | collective-permute-start | bytes 1572872 | tf_op jit(solution)/shard_map/ppermute | solution.py:78
  359.2 28.0 %collective-permute-start.48 = (bf16[512,256]{1,0:T(8,128)(2,1)}, bf16[512,256]{1,0:T(8,128)(2,1)}, u32[]{:S(2)}, u32[]{:S(2)}) collective-permute-start(bf16[512,256]{1,0:T(8,128)(2,1)} %get-tuple-element.482), channel_id=1, source_target_pairs={{0,2},{1,3},{2,4},{3,5},{4,6},{5,7},{6,0},{7,1},{8,10},{9,11},{10,... | collective-permute-start | bytes 786440 | tf_op jit(solution)/shard_map/ppermute | solution.py:67
  365.3 21.9 %collective-permute-start.49 = (bf16[512,256]{1,0:T(8,128)(2,1)}, bf16[512,256]{1,0:T(8,128)(2,1)}, u32[]{:S(2)}, u32[]{:S(2)}) collective-permute-start(bf16[512,256]{1,0:T(8,128)(2,1)} %get-tuple-element.483), channel_id=1, source_target_pairs={{0,4},{1,5},{2,6},{3,7},{4,0},{5,1},{6,2},{7,3},{8,12},{9,13},{10,... | collective-permute-start | bytes 786440 | tf_op jit(solution)/shard_map/ppermute | solution.py:67
  365.3 21.9 %collective-permute-start.50 = (bf16[512,256]{1,0:T(8,128)(2,1)}, bf16[512,256]{1,0:T(8,128)(2,1)}, u32[]{:S(2)}, u32[]{:S(2)}) collective-permute-start(bf16[512,256]{1,0:T(8,128)(2,1)} %get-tuple-element.484), channel_id=1, source_target_pairs={{0,6},{1,7},{2,0},{3,1},{4,2},{5,3},{6,4},{7,5},{8,14},{9,15},{10,... | collective-permute-start | bytes 786440 | tf_op jit(solution)/shard_map/ppermute | solution.py:67
  391.6 29.2 %collective-permute-start.54 = (bf16[2,4,128,256]{3,2,1,0:T(8,128)(2,1)S(1)}, bf16[2,4,128,256]{3,2,1,0:T(8,128)(2,1)}, u32[]{:S(2)}, u32[]{:S(2)}) collective-permute-start(bf16[2,4,128,256]{3,2,1,0:T(8,128)(2,1)S(1)} %get-tuple-element.511), channel_id=1, source_target_pairs={{0,8},{8,0},{16,24},{24,16},{1,9},{9,1},{17,25},{25,17},{2,10},{10... | collective-permute-start | bytes 1572872 | tf_op jit(solution)/shard_map/ppermute | solution.py:78
  392.3 28.5 %collective-permute-start.55 = (bf16[2,4,128,256]{3,2,1,0:T(8,128)(2,1)S(1)}, bf16[2,4,128,256]{3,2,1,0:T(8,128)(2,1)}, u32[]{:S(2)}, u32[]{:S(2)}) collective-permute-start(bf16[2,4,128,256]{3,2,1,0:T(8,128)(2,1)S(1)} %get-tuple-element.512), channel_id=1, source_target_pairs={{0,16},{8,24},{16,0},{24,8},{1,17},{9,25},{17,1},{25,9},{2,18},{10... | collective-permute-start | bytes 1572872 | tf_op jit(solution)/shard_map/ppermute | solution.py:78
  393.8 27.0 %collective-permute-start.51 = (bf16[256,512]{1,0:T(8,128)(2,1)}, bf16[256,512]{1,0:T(8,128)(2,1)S(1)}, u32[]{:S(2)}, u32[]{:S(2)}) collective-permute-start(bf16[256,512]{1,0:T(8,128)(2,1)} %get-tuple-element.508), channel_id=1, source_target_pairs={{0,2},{1,3},{2,4},{3,5},{4,6},{5,7},{6,0},{7,1},{8,10},{9,11},{10,... | collective-permute-start | bytes 786440 | tf_op jit(solution)/shard_map/ppermute | solution.py:67
  398.7 22.1 %collective-permute-start.52 = (bf16[256,512]{1,0:T(8,128)(2,1)}, bf16[256,512]{1,0:T(8,128)(2,1)S(1)}, u32[]{:S(2)}, u32[]{:S(2)}) collective-permute-start(bf16[256,512]{1,0:T(8,128)(2,1)} %get-tuple-element.509), channel_id=1, source_target_pairs={{0,4},{1,5},{2,6},{3,7},{4,0},{5,1},{6,2},{7,3},{8,12},{9,13},{10,... | collective-permute-start | bytes 786440 | tf_op jit(solution)/shard_map/ppermute | solution.py:67
  400.7 20.1 %collective-permute-start.53 = (bf16[256,512]{1,0:T(8,128)(2,1)}, bf16[256,512]{1,0:T(8,128)(2,1)}, u32[]{:S(2)}, u32[]{:S(2)}) collective-permute-start(bf16[256,512]{1,0:T(8,128)(2,1)} %get-tuple-element.510), channel_id=1, source_target_pairs={{0,6},{1,7},{2,0},{3,1},{4,2},{5,3},{6,4},{7,5},{8,14},{9,15},{10,... | collective-permute-start | bytes 786440 | tf_op jit(solution)/shard_map/ppermute | solution.py:67
  423.6 22.9 %collective-permute-start.57 = (bf16[1,128,1024]{2,1,0:T(8,128)(2,1)S(1)}, bf16[1,128,1024]{2,1,0:T(8,128)(2,1)S(1)}, u32[]{:S(2)}, u32[]{:S(2)}) collective-permute-start(bf16[1,128,1024]{2,1,0:T(8,128)(2,1)S(1)} %get-tuple-element.548), channel_id=1, source_target_pairs={{0,16},{8,24},{16,0},{24,8},{1,17},{9,25},{17,1},{25,9},{2,18},{10... | collective-permute-start | bytes 786440 | tf_op jit(solution)/shard_map/ppermute | solution.py:78
  423.6 23.8 %collective-permute-start.56 = (bf16[1,128,1024]{2,1,0:T(8,128)(2,1)S(1)}, bf16[1,128,1024]{2,1,0:T(8,128)(2,1)S(1)}, u32[]{:S(2)}, u32[]{:S(2)}) collective-permute-start(bf16[1,128,1024]{2,1,0:T(8,128)(2,1)S(1)} %get-tuple-element.547), channel_id=1, source_target_pairs={{0,8},{8,0},{16,24},{24,16},{1,9},{9,1},{17,25},{25,17},{2,10},{10... | collective-permute-start | bytes 786440 | tf_op jit(solution)/shard_map/ppermute | solution.py:78
  426.1 22.1 %collective-permute-start.58 = (bf16[1,4,128,256]{3,2,1,0:T(8,128)(2,1)S(1)}, bf16[1,4,128,256]{3,2,1,0:T(8,128)(2,1)S(1)}, u32[]{:S(2)}, u32[]{:S(2)}) collective-permute-start(bf16[1,4,128,256]{3,2,1,0:T(8,128)(2,1)S(1)} %slice.1123), channel_id=1, source_target_pairs={{0,16},{8,24},{16,0},{24,8},{1,17},{9,25},{17,1},{25,9},{2,18},{10... | collective-permute-start | bytes 786440 | tf_op jit(solution)/shard_map/ppermute | solution.py:78
  428.1 20.1 %collective-permute-start.59 = (bf16[1,4,128,256]{3,2,1,0:T(8,128)(2,1)S(1)}, bf16[1,4,128,256]{3,2,1,0:T(8,128)(2,1)S(1)}, u32[]{:S(2)}, u32[]{:S(2)}) collective-permute-start(bf16[1,4,128,256]{3,2,1,0:T(8,128)(2,1)S(1)} %slice.1124), channel_id=1, source_target_pairs={{0,8},{8,0},{16,24},{24,16},{1,9},{9,1},{17,25},{25,17},{2,10},{10... | collective-permute-start | bytes 786440 | tf_op jit(solution)/shard_map/ppermute | solution.py:78
  476.6 27.7 %collective-permute-start.73 = (bf16[2,128,1024]{2,1,0:T(8,128)(2,1)}, bf16[2,128,1024]{2,1,0:T(8,128)(2,1)}, u32[]{:S(2)}, u32[]{:S(2)}) collective-permute-start(bf16[2,128,1024]{2,1,0:T(8,128)(2,1)} %pad_maximum_fusion.13), channel_id=1, source_target_pairs={{0,8},{8,0},{16,24},{24,16},{1,9},{9,1},{17,25},{25,17},{2,10},{10... | collective-permute-start | bytes 1572872 | tf_op jit(solution)/shard_map/ppermute | solution.py:78
  477.8 27.8 %collective-permute-start.72 = (bf16[2,128,1024]{2,1,0:T(8,128)(2,1)}, bf16[2,128,1024]{2,1,0:T(8,128)(2,1)}, u32[]{:S(2)}, u32[]{:S(2)}) collective-permute-start(bf16[2,128,1024]{2,1,0:T(8,128)(2,1)} %pad_maximum_fusion.12), channel_id=1, source_target_pairs={{0,16},{8,24},{16,0},{24,8},{1,17},{9,25},{17,1},{25,9},{2,18},{10... | collective-permute-start | bytes 1572872 | tf_op jit(solution)/shard_map/ppermute | solution.py:78
  479.8 18.2 %collective-permute-start.67 = (bf16[1,4,128,256]{3,2,1,0:T(8,128)(2,1)}, bf16[1,4,128,256]{3,2,1,0:T(8,128)(2,1)}, u32[]{:S(2)}, u32[]{:S(2)}) collective-permute-start(bf16[1,4,128,256]{3,2,1,0:T(8,128)(2,1)} %slice.1127), channel_id=1, source_target_pairs={{0,16},{8,24},{16,0},{24,8},{1,17},{9,25},{17,1},{25,9},{2,18},{10... | collective-permute-start | bytes 786440 | tf_op jit(solution)/shard_map/ppermute | solution.py:78
  (136 other events, 1224.0 us)
